TPU v7x, 32 devices: a whole 2x2x4 slice. The times are simulated.
32 devices in a mesh: row: 4 (over z), col: 8 (over y, x, core).
Axes of the slice: x: 2, y: 2, z: 4, core: 2. Of those that a mesh axis runs over, the one named last changes fastest.
Arguments:
- object_field: bfloat16 [2, 2048, 4096], P(None, 'row', 'col'), may hold values from -6 to 6
- probe_modes: float32 [2, 2, 256, 256], replicated, may hold values from -6 to 6
- measured_amp: bfloat16 [4, 8, 8, 256, 256], P('row', 'col'), may hold values from 0.25 to 8
- scan_positions: int32 [4, 8, 2, 8], P('row', 'col'), may hold values from 0 to 512
- frame_counts: int32 [4, 8], P('row', 'col'), may hold values from 1 to 8, as said below
Outputs:
- object_grad: float32 [2, 2048, 4096], P(None, 'row', 'col')
- probe_grad: float32 [2, 2, 256, 256], replicated
Inputs may be any that keep to these rules, and one draw needn't show every extreme that they name: `frame_counts`: live frames of a tile; slots at or past it are ignored; some tile has exactly 8.
All inputs are finite; a program needn't handle non-finite values.
Results may differ from a plain program's by a relative error of at most 0.0059.
The roundings to bfloat16 on the way count: a program that leaves them out, or rounds other values in their place, can miss the bound.
Values may be sent and summed in bfloat16 or wider, within the bound.
A program may use at most 64 MiB of HBM per device.

v0:
```python
import math

import jax
import jax.numpy as jnp
from jax import lax
from jax.sharding import PartitionSpec as P

HALO = 128


def with_halo(value, sides, width):
    for axis, dim in sides:
        devices, length = (lax.axis_size(axis), value.shape[dim])
        up = [(i, (i + 1) % devices) for i in range(devices - 1)]
        down = [(j, i) for i, j in up]
        last = lax.slice_in_dim(value, length - width, length, axis=dim)
        leading = lax.slice_in_dim(value, 0, width, axis=dim)
        before = lax.ppermute(last, axis, up)
        after = lax.ppermute(leading, axis, down)
        value = jnp.concatenate([before, value, after], axis=dim)
    return value


def from_behind(value, axis, by):
    devices = lax.axis_size(axis)
    pairs = [(i, i + by) for i in range(devices) if 0 <= i + by < devices]
    return lax.ppermute(value, axis, pairs)


def fourier_tables(frame_side):
    indices = jnp.arange(frame_side, dtype=jnp.int32)
    product = indices[:, None] * indices[None, :] % frame_side
    angles = 2.0 * math.pi / frame_side * product.astype(jnp.float32)
    norm_scale = 1.0 / math.sqrt(frame_side)
    return (
        (jnp.cos(angles) * norm_scale).astype(jnp.bfloat16),
        (-jnp.sin(angles) * norm_scale).astype(jnp.bfloat16),
    )


def left_mul(table, data):
    return jnp.einsum("kn,mnj->mkj", table, data, preferred_element_type=jnp.float32)


def right_mul(data, table):
    return jnp.einsum("mkn,nj->mkj", data, table, preferred_element_type=jnp.float32)


def transform(real_part, imag_part, table_real, table_imag):
    first_real = (left_mul(table_real, real_part) - left_mul(table_imag, imag_part)).astype(
        jnp.bfloat16
    )
    first_imag = (left_mul(table_real, imag_part) + left_mul(table_imag, real_part)).astype(
        jnp.bfloat16
    )
    out_real = right_mul(first_real, table_real) - right_mul(first_imag, table_imag)
    out_imag = right_mul(first_real, table_imag) + right_mul(first_imag, table_real)
    return (out_real, out_imag)


def frame_terms(frame_patch, frame_amp, probe_modes, table_real, table_imag):
    probe_real = probe_modes[0]
    probe_imag = probe_modes[1]
    patch_real = frame_patch[0].astype(jnp.float32)
    patch_imag = frame_patch[1].astype(jnp.float32)
    exit_real = (probe_real * patch_real - probe_imag * patch_imag).astype(jnp.bfloat16)
    exit_imag = (probe_real * patch_imag + probe_imag * patch_real).astype(jnp.bfloat16)
    psi_real, psi_imag = transform(exit_real, exit_imag, table_real, table_imag)
    power = jnp.sum(psi_real * psi_real + psi_imag * psi_imag, axis=0)
    factor = 1.0 - frame_amp.astype(jnp.float32) / jnp.maximum(jnp.sqrt(power), 0.5)
    chi_real = (psi_real * factor).astype(jnp.bfloat16)
    chi_imag = (psi_imag * factor).astype(jnp.bfloat16)
    back_real, back_imag = transform(chi_real, chi_imag, table_real, -table_imag)
    patch_grad = jnp.stack(
        [
            jnp.sum(probe_real * back_real + probe_imag * back_imag, axis=0),
            jnp.sum(probe_real * back_imag - probe_imag * back_real, axis=0),
        ]
    )
    probe_term = jnp.stack(
        [
            patch_real * back_real + patch_imag * back_imag,
            patch_real * back_imag - patch_imag * back_real,
        ]
    )
    return (patch_grad, probe_term)


def shards(object_field, probe_modes, measured_amp, scan_positions, frame_counts):
    frame_side = probe_modes.shape[-1]
    slot_count = measured_amp.shape[2]
    tile_side = object_field.shape[1]
    extended = with_halo(object_field, (("row", 1), ("col", 2)), HALO)
    amplitudes = measured_amp[0, 0]
    row_starts = scan_positions[0, 0, 0]
    col_starts = scan_positions[0, 0, 1]
    live_count = frame_counts[0, 0]
    table_real, table_imag = fourier_tables(frame_side)

    def advance(slot_at, state_pair):
        gradient, probe_total = state_pair
        row_at = row_starts[slot_at]
        column_at = col_starts[slot_at]
        frame_patch = lax.dynamic_slice(
            extended, (0, row_at, column_at), (2, frame_side, frame_side)
        )
        frame_amp = lax.dynamic_index_in_dim(amplitudes, slot_at, 0, keepdims=False)
        patch_grad, probe_term = frame_terms(
            frame_patch, frame_amp, probe_modes, table_real, table_imag
        )
        old_block = lax.dynamic_slice(gradient, (0, row_at, column_at), (2, frame_side, frame_side))
        gradient = lax.dynamic_update_slice(
            gradient, old_block + patch_grad, (0, row_at, column_at)
        )
        return (gradient, probe_total + probe_term)

    gradient = jnp.zeros((2, tile_side + 2 * HALO, tile_side + 2 * HALO), jnp.float32)
    probe_zero = jnp.zeros(probe_modes.shape, jnp.float32)
    gradient, probe_local = lax.fori_loop(
        jnp.zeros((), jnp.int32), live_count, advance, (gradient, probe_zero)
    )
    low_end = tile_side + HALO
    from_above = from_behind(gradient[:, low_end:, :].astype(jnp.bfloat16), "row", 1).astype(
        jnp.float32
    )
    from_below = from_behind(gradient[:, :HALO, :].astype(jnp.bfloat16), "row", -1).astype(
        jnp.float32
    )
    middle = gradient[:, HALO:low_end, :]
    middle = middle.at[:, :HALO, :].add(from_above)
    middle = middle.at[:, tile_side - HALO :, :].add(from_below)
    from_left = from_behind(middle[:, :, low_end:].astype(jnp.bfloat16), "col", 1).astype(
        jnp.float32
    )
    from_right = from_behind(middle[:, :, :HALO].astype(jnp.bfloat16), "col", -1).astype(
        jnp.float32
    )
    interior = middle[:, :, HALO:low_end]
    interior = interior.at[:, :, :HALO].add(from_left)
    interior = interior.at[:, :, tile_side - HALO :].add(from_right)
    probe_total = lax.psum(probe_local, ("row", "col"))
    norm_scale = 1.0 / math.sqrt(lax.axis_size("row") * lax.axis_size("col") * slot_count)
    return (interior, probe_total * norm_scale)


def solution(mesh):
    in_specs = (
        P(None, "row", "col"),
        P(),
        P("row", "col", None, None, None),
        P("row", "col", None, None),
        P("row", "col"),
    )
    out_specs = (P(None, "row", "col"), P())
    return jax.shard_map(shards, mesh=mesh, in_specs=in_specs, out_specs=out_specs, check_vma=False)
```

profile of v0, /device:TPU:0, one launch (start us, length us, event | category | flops | bytes accessed | tf_op | source)
XLA Modules:
  0.0 478.8 jit_solution(10748043723370413190)
XLA Ops:
  8.3 5.0 %collective-permute-start = (bf16[2,128,512]{2,1,0:T(8,128)(2,1)S(1)}, bf16[2,128,512]{2,1,0:T(8,128)(2,1)S(1)}, u32[]{:S(2)}, u32[]{:S(2)}) collective-permute-start(bf16[2,128,512]{2,1,0:T(8,128)(2,1)S(1)} %get-tuple-element.305), channel_id=1, source_target_pairs={{0,8},{8,16},{16,24},{1,9},{9,17},{17,25},{2,10},{10,18},{18,26},{... | collective-permute-start | bytes 786440 | tf_op jit(solution)/shard_map/ppermute | solution.py:18
  13.3 1.3 collective-permute-start.1
  14.6 4.2 collective-permute-done
  18.8 1.3 constant_dynamic-update-slice_fusion.1
  20.1 2.8 collective-permute-done.1
  23.1 1.3 collective-permute-start.2
  24.4 1.3 collective-permute-start.3
  25.8 4.0 collective-permute-done.3
  29.7 1.7 pad_maximum_fusion
  31.5 2.4 broadcast_in_dim.4
  33.9 144.1 %while.19 = (s32[]{:T(128)}, f32[2,768,768]{2,1,0:T(8,128)}, f32[2,2,256,256]{3,2,1,0:T(8,128)S(1)}, s32[]{:T(128)}, s32[8]{0:T(128)S(1)}, /*index=5*/s32[8]{0:T...) while((s32[]{:T(128)}, f32[2,768,768]{2,1,0:T(8,128)}, ...), condition=%wide.region_4.5_spmd.clone.clone, body=%wide.region_0.4_spmd.clone.clone.sunk | while | flops 1098842112 | bytes 31064372 | solution.py:119
  39.7 1.2 fusion.232
  48.2 1.2 convolution_subtract_fusion.5
  49.4 1.2 add_reduce_fusion.2
  51.6 1.2 fusion.244
  52.8 1.2 fusion.245
  54.0 1.2 fusion.241
  55.2 1.2 fusion.242
  60.1 1.4 add_bitcast_fusion.2
  61.5 1.4 maximum_add_fusion.4
  63.1 6.5 %dynamic_update_slice.7 = f32[2,768,768]{2,1,0:T(8,128)} dynamic-update-slice(f32[2,768,768]{2,1,0:T(8,128)} %get-tuple-element.399, f32[2,256,256]{2,1,0:T(8,128)S(1)} %maximum_add_fusion.4, s32[]{:T(128)} %constant.148.clone.1..sunk, s32[]{:T(128)S(6)} %select_n.158, s32[]{:T(128)S(6)} %select_n.159) | dynamic-update-slice | bytes 1048580 | tf_op jit(solution)/shard_map/while/body/dynamic_update_slice | solution.py:112
  75.3 1.2 fusion.232
  83.8 1.2 convolution_subtract_fusion.5
  85.0 1.2 add_reduce_fusion.2
  87.3 1.2 fusion.244
  88.5 1.2 fusion.245
  89.7 1.2 fusion.241
  90.9 1.2 fusion.242
  95.7 1.4 add_bitcast_fusion.2
  97.1 1.4 maximum_add_fusion.4
  98.7 6.8 %dynamic_update_slice.7 = f32[2,768,768]{2,1,0:T(8,128)} dynamic-update-slice(f32[2,768,768]{2,1,0:T(8,128)} %get-tuple-element.399, f32[2,256,256]{2,1,0:T(8,128)S(1)} %maximum_add_fusion.4, s32[]{:T(128)} %constant.148.clone.1..sunk, s32[]{:T(128)S(6)} %select_n.158, s32[]{:T(128)S(6)} %select_n.159) | dynamic-update-slice | bytes 1048580 | tf_op jit(solution)/shard_map/while/body/dynamic_update_slice | solution.py:112
  111.3 1.2 fusion.232
  119.8 1.2 convolution_subtract_fusion.5
  121.0 1.2 add_reduce_fusion.2
  123.2 1.2 fusion.244
  124.4 1.2 fusion.245
  125.6 1.2 fusion.241
  126.8 1.2 fusion.242
  131.6 1.4 add_bitcast_fusion.2
  133.0 1.4 maximum_add_fusion.4
  134.7 6.8 %dynamic_update_slice.7 = f32[2,768,768]{2,1,0:T(8,128)} dynamic-update-slice(f32[2,768,768]{2,1,0:T(8,128)} %get-tuple-element.399, f32[2,256,256]{2,1,0:T(8,128)S(1)} %maximum_add_fusion.4, s32[]{:T(128)} %constant.148.clone.1..sunk, s32[]{:T(128)S(6)} %select_n.158, s32[]{:T(128)S(6)} %select_n.159) | dynamic-update-slice | bytes 1048580 | tf_op jit(solution)/shard_map/while/body/dynamic_update_slice | solution.py:112
  147.2 1.2 fusion.232
  155.7 1.2 convolution_subtract_fusion.5
  156.9 1.2 add_reduce_fusion.2
  159.1 1.2 fusion.244
  160.3 1.2 fusion.245
  162.8 1.2 fusion.242
  167.6 1.4 add_bitcast_fusion.2
  169.0 1.4 maximum_add_fusion.4
  170.6 6.8 %dynamic_update_slice.7 = f32[2,768,768]{2,1,0:T(8,128)} dynamic-update-slice(f32[2,768,768]{2,1,0:T(8,128)} %get-tuple-element.399, f32[2,256,256]{2,1,0:T(8,128)S(1)} %maximum_add_fusion.4, s32[]{:T(128)} %constant.148.clone.1..sunk, s32[]{:T(128)S(6)} %select_n.158, s32[]{:T(128)S(6)} %select_n.159) | dynamic-update-slice | bytes 1048580 | tf_op jit(solution)/shard_map/while/body/dynamic_update_slice | solution.py:112
  178.1 3.0 convert.10
  181.1 73.0 %collective-permute-start.4 = (bf16[2,128,768]{2,1,0:T(8,128)(2,1)S(1)}, bf16[2,128,768]{2,1,0:T(8,128)(2,1)S(1)}, u32[]{:S(2)}, u32[]{:S(2)}) collective-permute-start(bf16[2,128,768]{2,1,0:T(8,128)(2,1)S(1)} %get-tuple-element.299), channel_id=1, source_target_pairs={{0,8},{8,16},{16,24},{1,9},{9,17},{17,25},{2,10},{10,18},{18,26},{... | collective-permute-start | bytes 1179656 | tf_op jit(solution)/shard_map/ppermute | solution.py:27
  254.2 1.3 collective-permute-start.5
  255.5 1.8 slice.160
  257.4 2.1 collective-permute-done.4
  259.4 2.1 add_dynamic-update-slice_fusion
  261.6 74.4 %collective-permute-done.5 = bf16[2,128,768]{2,1,0:T(8,128)(2,1)S(1)} collective-permute-done((bf16[2,128,768]{2,1,0:T(8,128)(2,1)S(1)}, bf16[2,128,768]{2,1,0:T(8,128)(2,1)S(1)}, u32[]{:S(2)}, u32[]{:S(2)}) %collective-permute-start.5) | collective-permute-done | bytes 393248 | tf_op jit(solution)/shard_map/ppermute | solution.py:27
  335.9 2.1 fusion.142
  338.0 2.2 convert.11
  341.2 1.3 collective-permute-start.7
  342.5 7.6 %collective-permute-start.6 = (bf16[2,512,128]{2,1,0:T(8,128)(2,1)S(1)}, bf16[2,512,128]{2,1,0:T(8,128)(2,1)S(1)}, u32[]{:S(2)}, u32[]{:S(2)}) collective-permute-start(bf16[2,512,128]{2,1,0:T(8,128)(2,1)S(1)} %get-tuple-element.301), channel_id=1, source_target_pairs={{0,1},{1,2},{2,3},{3,4},{4,5},{5,6},{6,7},{8,9},{9,10},{10,11},{11... | collective-permute-start | bytes 786440 | tf_op jit(solution)/shard_map/ppermute | solution.py:27
  350.2 116.9 %all-reduce.2.cloned.1.call-done = f32[2,2,256,256]{3,2,1,0:T(8,128)} async-done(((f32[2,2,256,256]{3,2,1,0:T(8,128)}), f32[2,2,256,256]{3,2,1,0:T(8,128)}) %all-reduce.2.cloned.1.call-update) | async-done | bytes 1048592 | tf_op jit(solution)/shard_map/psum | solution.py:141
  467.1 2.3 broadcast_multiply_fusion
  470.6 1.3 copy-done.4
  (84 shorter events, 58.0 us)
Async XLA Ops:
  7.2 459.9 %all-reduce.2.cloned.1.call-start = ((), (), s32[]{:S(2)}) async-start(), calls=%async_computation | async-start | bytes 2097152 | tf_op jit(solution)/shard_map/psum | solution.py:141
  8.3 10.5 %collective-permute-start = (bf16[2,128,512]{2,1,0:T(8,128)(2,1)S(1)}, bf16[2,128,512]{2,1,0:T(8,128)(2,1)S(1)}, u32[]{:S(2)}, u32[]{:S(2)}) collective-permute-start(bf16[2,128,512]{2,1,0:T(8,128)(2,1)S(1)} %get-tuple-element.305), channel_id=1, source_target_pairs={{0,8},{8,16},{16,24},{1,9},{9,17},{17,25},{2,10},{10,18},{18,26},{... | collective-permute-start | bytes 786440 | tf_op jit(solution)/shard_map/ppermute | solution.py:18
  13.3 12.5 %copy-start.5 = (s32[1,1,2,8]{3,2,1,0:T(2,128)S(1)}, s32[1,1,2,8]{3,2,1,0:T(2,128)}, u32[]{:S(2)}) copy-start(s32[1,1,2,8]{3,2,1,0:T(2,128)} %param.18) | copy-start | bytes 196
  13.3 9.7 %collective-permute-start.1 = (bf16[2,128,512]{2,1,0:T(8,128)(2,1)S(1)}, bf16[2,128,512]{2,1,0:T(8,128)(2,1)S(1)}, u32[]{:S(2)}, u32[]{:S(2)}) collective-permute-start(bf16[2,128,512]{2,1,0:T(8,128)(2,1)S(1)} %get-tuple-element.304), channel_id=1, source_target_pairs={{8,0},{16,8},{24,16},{9,1},{17,9},{25,17},{10,2},{18,10},{26,18},{... | collective-permute-start | bytes 786440 | tf_op jit(solution)/shard_map/ppermute | solution.py:19
  23.1 2.6 collective-permute-start.2
  24.4 5.3 %collective-permute-start.3 = (bf16[2,768,128]{2,1,0:T(8,128)(2,1)S(1)}, bf16[2,768,128]{2,1,0:T(8,128)(2,1)S(1)}, u32[]{:S(2)}, u32[]{:S(2)}) collective-permute-start(bf16[2,768,128]{2,1,0:T(8,128)(2,1)S(1)} %get-tuple-element.303), channel_id=1, source_target_pairs={{1,0},{2,1},{3,2},{4,3},{5,4},{6,5},{7,6},{9,8},{10,9},{11,10},{12... | collective-permute-start | bytes 1179656 | tf_op jit(solution)/shard_map/ppermute | solution.py:19
  31.5 2.4 copy-start
  178.1 3.0 copy-start.2
  178.1 77.4 %copy-start.1 = (f32[2,768,768]{2,1,0:T(8,128)S(1)}, f32[2,768,768]{2,1,0:T(8,128)}, u32[]{:S(2)}) copy-start(f32[2,768,768]{2,1,0:T(8,128)} %get-tuple-element.198) | copy-start | bytes 14155780
  181.1 78.3 %collective-permute-start.4 = (bf16[2,128,768]{2,1,0:T(8,128)(2,1)S(1)}, bf16[2,128,768]{2,1,0:T(8,128)(2,1)S(1)}, u32[]{:S(2)}, u32[]{:S(2)}) collective-permute-start(bf16[2,128,768]{2,1,0:T(8,128)(2,1)S(1)} %get-tuple-element.299), channel_id=1, source_target_pairs={{0,8},{8,16},{16,24},{1,9},{9,17},{17,25},{2,10},{10,18},{18,26},{... | collective-permute-start | bytes 1179656 | tf_op jit(solution)/shard_map/ppermute | solution.py:27
  254.2 81.8 %collective-permute-start.5 = (bf16[2,128,768]{2,1,0:T(8,128)(2,1)S(1)}, bf16[2,128,768]{2,1,0:T(8,128)(2,1)S(1)}, u32[]{:S(2)}, u32[]{:S(2)}) collective-permute-start(bf16[2,128,768]{2,1,0:T(8,128)(2,1)S(1)} %get-tuple-element.298), channel_id=1, source_target_pairs={{8,0},{16,8},{24,16},{9,1},{17,9},{25,17},{10,2},{18,10},{26,18},{... | collective-permute-start | bytes 1179656 | tf_op jit(solution)/shard_map/ppermute | solution.py:27
  338.0 2.8 copy-start.3
  341.2 129.3 %collective-permute-start.7 = (bf16[2,512,128]{2,1,0:T(8,128)(2,1)S(1)}, bf16[2,512,128]{2,1,0:T(8,128)(2,1)S(1)}, u32[]{:S(2)}, u32[]{:S(2)}) collective-permute-start(bf16[2,512,128]{2,1,0:T(8,128)(2,1)S(1)} %get-tuple-element.300), channel_id=1, source_target_pairs={{1,0},{2,1},{3,2},{4,3},{5,4},{6,5},{7,6},{9,8},{10,9},{11,10},{12... | collective-permute-start | bytes 786440 | tf_op jit(solution)/shard_map/ppermute | solution.py:27
  342.5 126.8 %collective-permute-start.6 = (bf16[2,512,128]{2,1,0:T(8,128)(2,1)S(1)}, bf16[2,512,128]{2,1,0:T(8,128)(2,1)S(1)}, u32[]{:S(2)}, u32[]{:S(2)}) collective-permute-start(bf16[2,512,128]{2,1,0:T(8,128)(2,1)S(1)} %get-tuple-element.301), channel_id=1, source_target_pairs={{0,1},{1,2},{2,3},{3,4},{4,5},{5,6},{6,7},{8,9},{9,10},{10,11},{11... | collective-permute-start | bytes 786440 | tf_op jit(solution)/shard_map/ppermute | solution.py:27
  470.6 1.3 copy-start.4
Sparse Core Ops, SparseCore 0:
  257.5 209.5 all-reduce.1
where the time goes:
time: 482 us; the launch traced here: 479 us
  waiting for transfers between devices  204 us (42%)
  starting transfers between devices  92.2 us (19%)
  matrix products  77.3 us (16%)
  local copies, waits for them, and re-layouts  40.8 us (8%)
  other arithmetic  30.5 us (6%)
  loops' own time  19.2 us (4%)
  between operations  14.3 us (3%)
    psum x1, waiting for transfers between devices, shards(): probe_total = lax.psum(probe_local, ('row', 'col'))  117 us
    ppermute x4, starting transfers between devices, from_behind(): return lax.ppermute(value, axis, pairs)  83.3 us
    ppermute x4, waiting for transfers between devices, from_behind(): return lax.ppermute(value, axis, pairs)  76.5 us
    dot_general x32, matrix products, right_mul(): jnp.einsum('mkn,nj->mkj', data, table, preferred_element_type=jnp.float32)  39.1 us
    dot_general x32, matrix products, left_mul(): jnp.einsum('kn,mnj->mkj', table, data, preferred_element_type=jnp.float32)  38.2 us
    dynamic_update_slice x4, local copies, waits for them, and re-layouts, advance(): lax.dynamic_update_slice(gradient, old_block + patch_grad, (0, row_at, co...  26.8 us
    another operation x1, loops' own time, shards(): lax.fori_loop(jnp.zeros((), jnp.int32), live_count, advance, (gradient, p...  19.2 us
  transfers between devices with their start and end apart: 9, of which 6 were waited for; matrix products, arithmetic and copies ran while one was open for 3% of the time, Pallas kernels for 0%

commit v1 on v0

v1 whole, which is shorter than its diff:
```python
import math

import jax
import jax.numpy as jnp
from jax import lax
from jax.experimental import pallas as pl
from jax.experimental.pallas import tpu as pltpu
from jax.sharding import PartitionSpec as P

HALO = 128


def with_halo(value, sides, width):
    for axis, dim in sides:
        devices, length = (lax.axis_size(axis), value.shape[dim])
        up = [(i, (i + 1) % devices) for i in range(devices - 1)]
        down = [(j, i) for i, j in up]
        last = lax.slice_in_dim(value, length - width, length, axis=dim)
        leading = lax.slice_in_dim(value, 0, width, axis=dim)
        before = lax.ppermute(last, axis, up)
        after = lax.ppermute(leading, axis, down)
        value = jnp.concatenate([before, value, after], axis=dim)
    return value


def from_behind(value, axis, by):
    devices = lax.axis_size(axis)
    pairs = [(i, i + by) for i in range(devices) if 0 <= i + by < devices]
    return lax.ppermute(value, axis, pairs)


def fourier_tables(frame_side):
    indices = jnp.arange(frame_side, dtype=jnp.int32)
    product = indices[:, None] * indices[None, :] % frame_side
    angles = 2.0 * math.pi / frame_side * product.astype(jnp.float32)
    norm_scale = 1.0 / math.sqrt(frame_side)
    return (
        (jnp.cos(angles) * norm_scale).astype(jnp.bfloat16),
        (-jnp.sin(angles) * norm_scale).astype(jnp.bfloat16),
    )


LANES = 128
CHUNK = 32


def dot32(left, right):
    return jnp.dot(left, right, preferred_element_type=jnp.float32)


def frames_kernel(
    count_ref, at_ref, ext_ref, probe_ref, amp_ref, tr_ref, ti_ref, acc_ref, pacc_ref,
    extf, fwd, inv, stage, half, wide, patch,
):
    fs = probe_ref.shape[-1]
    modes = probe_ref.shape[1]
    tiles = ext_ref.shape[2] // LANES
    lane_tiles = fs // LANES
    for plane in range(2):
        for t in range(tiles):
            extf[plane, t] = ext_ref[plane, :, t * LANES : (t + 1) * LANES].astype(jnp.float32)
        extf[plane, tiles] = jnp.zeros(extf.shape[2:], jnp.float32)
    acc_ref[...] = jnp.zeros(acc_ref.shape, jnp.float32)
    pacc_ref[...] = jnp.zeros(pacc_ref.shape, jnp.float32)
    table_real, table_imag = tr_ref[...], ti_ref[...]
    minus = -table_imag
    fwd[:fs, :fs] = table_real
    fwd[:fs, fs:] = minus
    fwd[fs:, :fs] = table_imag
    fwd[fs:, fs:] = table_real
    inv[:fs, :fs] = table_real
    inv[:fs, fs:] = table_imag
    inv[fs:, :fs] = minus
    inv[fs:, fs:] = table_real

    def two_sided(left_table, right_table):
        for m in range(modes):
            both = dot32(left_table[...], stage[:, m * fs : (m + 1) * fs])
            half[m * fs : (m + 1) * fs, :fs] = both[:fs].astype(jnp.bfloat16)
            half[m * fs : (m + 1) * fs, fs:] = both[fs:].astype(jnp.bfloat16)
        wide[...] = dot32(half[...], right_table[...])

    def advance(slot, carry):
        row_at = at_ref[0, slot]
        col_at = at_ref[1, slot]
        tile_at = col_at // LANES
        shift = col_at % LANES
        back_shift = (LANES - shift) % LANES
        lane = lax.broadcasted_iota(jnp.int32, (CHUNK, LANES), 1)
        keep_low = lane < LANES - shift
        from_same = lane >= shift
        for r in range(0, fs, CHUNK):
            rows = slice(r, r + CHUNK)
            values = []
            for plane in range(2):
                rolled = [
                    pltpu.roll(
                        extf[plane, tile_at + t, pl.ds(row_at + r, CHUNK), :], back_shift, 1
                    )
                    for t in range(lane_tiles + 1)
                ]
                values.append(
                    [jnp.where(keep_low, rolled[t], rolled[t + 1]) for t in range(lane_tiles)]
                )
            for t in range(lane_tiles):
                cols = slice(t * LANES, (t + 1) * LANES)
                patch_real, patch_imag = values[0][t], values[1][t]
                patch[0, rows, cols] = patch_real
                patch[1, rows, cols] = patch_imag
                for m in range(modes):
                    probe_real = probe_ref[0, m, rows, cols]
                    probe_imag = probe_ref[1, m, rows, cols]
                    out = slice(m * fs + t * LANES, m * fs + (t + 1) * LANES)
                    stage[rows, out] = (
                        probe_real * patch_real - probe_imag * patch_imag
                    ).astype(jnp.bfloat16)
                    stage[fs + r : fs + r + CHUNK, out] = (
                        probe_real * patch_imag + probe_imag * patch_real
                    ).astype(jnp.bfloat16)
        two_sided(fwd, inv)
        for r in range(0, fs, CHUNK):
            for t in range(lane_tiles):
                cols = slice(t * LANES, (t + 1) * LANES)
                imag_cols = slice(fs + t * LANES, fs + (t + 1) * LANES)
                psi = []
                power = jnp.zeros((CHUNK, LANES), jnp.float32)
                for m in range(modes):
                    rows = slice(m * fs + r, m * fs + r + CHUNK)
                    real, imag = wide[rows, cols], wide[rows, imag_cols]
                    psi.append((real, imag))
                    power = power + (real * real + imag * imag)
                amp = amp_ref[slot, r : r + CHUNK, cols].astype(jnp.float32)
                factor = 1.0 - amp * lax.rsqrt(jnp.maximum(power, 0.25))
                for m in range(modes):
                    out = slice(m * fs + t * LANES, m * fs + (t + 1) * LANES)
                    stage[r : r + CHUNK, out] = (psi[m][0] * factor).astype(jnp.bfloat16)
                    stage[fs + r : fs + r + CHUNK, out] = (psi[m][1] * factor).astype(jnp.bfloat16)
        two_sided(inv, fwd)
        for r in range(0, fs, CHUNK):
            grads = [[], []]
            for t in range(lane_tiles):
                cols = slice(t * LANES, (t + 1) * LANES)
                imag_cols = slice(fs + t * LANES, fs + (t + 1) * LANES)
                patch_real = patch[0, r : r + CHUNK, cols]
                patch_imag = patch[1, r : r + CHUNK, cols]
                total_real = total_imag = 0.0
                for m in range(modes):
                    rows = slice(m * fs + r, m * fs + r + CHUNK)
                    real, imag = wide[rows, cols], wide[rows, imag_cols]
                    probe_real = probe_ref[0, m, r : r + CHUNK, cols]
                    probe_imag = probe_ref[1, m, r : r + CHUNK, cols]
                    total_real = total_real + (probe_real * real + probe_imag * imag)
                    total_imag = total_imag + (probe_real * imag - probe_imag * real)
                    at = (m * lane_tiles + t) * fs + r
                    pacc_ref[at : at + CHUNK, :] += patch_real * real + patch_imag * imag
                    at += modes * lane_tiles * fs
                    pacc_ref[at : at + CHUNK, :] += patch_real * imag - patch_imag * real
                grads[0].append(pltpu.roll(total_real, shift, 1))
                grads[1].append(pltpu.roll(total_imag, shift, 1))
            for plane in range(2):
                rolled = grads[plane]
                for t in range(lane_tiles + 1):
                    same = rolled[t] if t < lane_tiles else 0.0
                    before = rolled[t - 1] if t > 0 else 0.0
                    where = (plane, tile_at + t, pl.ds(row_at + r, CHUNK), slice(None))
                    acc_ref[where] += jnp.where(from_same, same, before)
        return carry

    lax.fori_loop(0, count_ref[0], advance, 0)


def frames_call(extended, probe_modes, amplitudes, positions, live_count, tables):
    fs = probe_modes.shape[-1]
    modes = probe_modes.shape[1]
    ext_rows, ext_cols = extended.shape[1:]
    tiled = (2, ext_cols // LANES + 1, ext_rows, LANES)
    vmem = pl.BlockSpec(memory_space=pltpu.VMEM)
    smem = pl.BlockSpec(memory_space=pltpu.SMEM)
    return pl.pallas_call(
        frames_kernel,
        out_shape=(
            jax.ShapeDtypeStruct(tiled, jnp.float32),
            jax.ShapeDtypeStruct((probe_modes.size // LANES, LANES), jnp.float32),
        ),
        in_specs=[smem, smem, vmem, vmem, vmem, vmem, vmem],
        out_specs=(vmem, vmem),
        scratch_shapes=[
            pltpu.VMEM(tiled, jnp.float32),
            pltpu.VMEM((2 * fs, 2 * fs), jnp.bfloat16),
            pltpu.VMEM((2 * fs, 2 * fs), jnp.bfloat16),
            pltpu.VMEM((2 * fs, modes * fs), jnp.bfloat16),
            pltpu.VMEM((modes * fs, 2 * fs), jnp.bfloat16),
            pltpu.VMEM((modes * fs, 2 * fs), jnp.float32),
            pltpu.VMEM((2, fs, fs), jnp.float32),
        ],
        compiler_params=pltpu.CompilerParams(vmem_limit_bytes=56 * 1024 * 1024),
        name="frames",
    )(live_count.reshape(1), positions, extended, probe_modes, amplitudes, *tables)


def shards(object_field, probe_modes, measured_amp, scan_positions, frame_counts):
    frame_side = probe_modes.shape[-1]
    slot_count = measured_amp.shape[2]
    tile_side = object_field.shape[1]
    extended = with_halo(object_field, (("row", 1), ("col", 2)), HALO)
    amplitudes = measured_amp[0, 0]
    acc, probe_flat = frames_call(
        extended,
        probe_modes,
        amplitudes,
        scan_positions[0, 0],
        frame_counts[0, 0],
        fourier_tables(frame_side),
    )
    gradient = acc[:, :-1].transpose(0, 2, 1, 3).reshape(extended.shape)
    modes = probe_modes.shape[1]
    probe_local = probe_flat.reshape(2, modes, frame_side // LANES, frame_side, LANES)
    probe_local = probe_local.transpose(0, 1, 3, 2, 4).reshape(probe_modes.shape)
    low_end = tile_side + HALO
    from_above = from_behind(gradient[:, low_end:, :].astype(jnp.bfloat16), "row", 1).astype(
        jnp.float32
    )
    from_below = from_behind(gradient[:, :HALO, :].astype(jnp.bfloat16), "row", -1).astype(
        jnp.float32
    )
    middle = gradient[:, HALO:low_end, :]
    middle = middle.at[:, :HALO, :].add(from_above)
    middle = middle.at[:, tile_side - HALO :, :].add(from_below)
    from_left = from_behind(middle[:, :, low_end:].astype(jnp.bfloat16), "col", 1).astype(
        jnp.float32
    )
    from_right = from_behind(middle[:, :, :HALO].astype(jnp.bfloat16), "col", -1).astype(
        jnp.float32
    )
    interior = middle[:, :, HALO:low_end]
    interior = interior.at[:, :, :HALO].add(from_left)
    interior = interior.at[:, :, tile_side - HALO :].add(from_right)
    probe_total = lax.psum(probe_local, ("row", "col"))
    norm_scale = 1.0 / math.sqrt(lax.axis_size("row") * lax.axis_size("col") * slot_count)
    return (interior, probe_total * norm_scale)


def solution(mesh):
    in_specs = (
        P(None, "row", "col"),
        P(),
        P("row", "col", None, None, None),
        P("row", "col", None, None),
        P("row", "col"),
    )
    out_specs = (P(None, "row", "col"), P())
    return jax.shard_map(shards, mesh=mesh, in_specs=in_specs, out_specs=out_specs, check_vma=False)
```

time: 482 us -> 229 us (0.48)
  matrix products: 77.3 us -> 0 us
  starting transfers between devices: 92.2 us -> 25.2 us
  waiting for transfers between devices: 204 us -> 137 us
  loops' own time: 19.2 us -> 0 us
  local copies, waits for them, and re-layouts: 40.8 us -> 22.8 us
  other arithmetic: 30.5 us -> 14.8 us
  Pallas kernels: 0 us -> 14.5 us
    dot_general x64 -> x0, matrix products: 77.3 us -> none  [the longest x32 39.1 us: right_mul(): jnp.einsum('mkn,nj->mkj', data, table, preferred_element_type=jnp.float32)]
    ppermute x4, waiting for transfers between devices: 76.5 us -> 6.89 us  [from_behind(): return lax.ppermute(value, axis, pairs)]
    ppermute x4, starting transfers between devices: 83.3 us -> 16.3 us  [from_behind(): return lax.ppermute(value, axis, pairs)]
    dynamic_update_slice x4 -> x0, local copies, waits for them, and re-layouts: 26.8 us -> none  [advance(): lax.dynamic_update_slice(gradient, old_block + patch_grad, (0, row_at, co...]
    another operation x1 -> x0, loops' own time: 19.2 us -> none  [shards(): lax.fori_loop(jnp.zeros((), jnp.int32), live_count, advance, (gradient, p...]
    pallas_call x0 -> x1, Pallas kernels: none -> 14.5 us  [frames_call(): pl.pallas_call(frames_kernel, out_shape=(jax.ShapeDtypeStruct(tiled, jnp....]
    transpose x0 -> x2, local copies, waits for them, and re-layouts: none -> 10.9 us  [shards(): gradient = acc[:, :-1].transpose(0, 2, 1, 3).reshape(extended.shape)]
    mul x8 -> x0, other arithmetic: 8.97 us -> none  [the longest x4 4.87 us: frame_terms(): probe_real * patch_real - probe_imag * patch_imag]
  transfers between devices with their start and end apart: 9 -> 9, of which waited for: 6 -> 6; matrix products, arithmetic and copies ran while one was open for 3% -> 7% of each run, Pallas kernels for 0% -> 0%
where the time goes in v1:
time: 229 us
  waiting for transfers between devices  137 us (60%)
  starting transfers between devices  25.2 us (11%)
  local copies, waits for them, and re-layouts  22.8 us (10%)
  other arithmetic  14.8 us (6%)
  between operations  14.8 us (6%)
  Pallas kernels  14.5 us (6%)
    psum x1, waiting for transfers between devices, shards(): probe_total = lax.psum(probe_local, ('row', 'col'))  121 us
    ppermute x4, starting transfers between devices, from_behind(): return lax.ppermute(value, axis, pairs)  16.3 us
    pallas_call x1, Pallas kernels, frames_call(): pl.pallas_call(frames_kernel, out_shape=(jax.ShapeDtypeStruct(tiled, jnp....  14.5 us
    transpose x2, local copies, waits for them, and re-layouts, shards(): gradient = acc[:, :-1].transpose(0, 2, 1, 3).reshape(extended.shape)  10.9 us
    ppermute x4, waiting for transfers between devices, from_behind(): return lax.ppermute(value, axis, pairs)  6.89 us
    ppermute x2, starting transfers between devices, with_halo(): before = lax.ppermute(last, axis, up)  6.29 us
  transfers between devices with their start and end apart: 9, of which 6 were waited for; matrix products, arithmetic and copies ran while one was open for 7% of the time, Pallas kernels for 0%

profile of v1, /device:TPU:0, one launch (start us, length us, event | category | flops | bytes accessed | tf_op | source)
XLA Modules:
  0.0 228.5 jit_solution(8313840582941586259)
XLA Ops:
  7.2 0.0 all-reduce.2.cloned.1.call-start
  7.2 1.1 fusion.13
  8.3 5.0 %collective-permute-start = (bf16[2,128,512]{2,1,0:T(8,128)(2,1)S(1)}, bf16[2,128,512]{2,1,0:T(8,128)(2,1)S(1)}, u32[]{:S(2)}, u32[]{:S(2)}) collective-permute-start(bf16[2,128,512]{2,1,0:T(8,128)(2,1)S(1)} %get-tuple-element.63), channel_id=1, source_target_pairs={{0,8},{8,16},{16,24},{1,9},{9,17},{17,25},{2,10},{10,18},{18,26},{... | collective-permute-start | bytes 786440 | tf_op jit(solution)/shard_map/ppermute | solution.py:20
  13.3 1.3 collective-permute-start.1
  14.6 4.2 %collective-permute-done = bf16[2,128,512]{2,1,0:T(8,128)(2,1)S(1)} collective-permute-done((bf16[2,128,512]{2,1,0:T(8,128)(2,1)S(1)}, bf16[2,128,512]{2,1,0:T(8,128)(2,1)S(1)}, u32[]{:S(2)}, u32[]{:S(2)}) %collective-permute-start) | collective-permute-done | bytes 262176 | tf_op jit(solution)/shard_map/ppermute | solution.py:20
  18.8 1.3 constant_dynamic-update-slice_fusion.1
  20.1 2.8 %collective-permute-done.1 = bf16[2,128,512]{2,1,0:T(8,128)(2,1)S(1)} collective-permute-done((bf16[2,128,512]{2,1,0:T(8,128)(2,1)S(1)}, bf16[2,128,512]{2,1,0:T(8,128)(2,1)S(1)}, u32[]{:S(2)}, u32[]{:S(2)}) %collective-permute-start.1) | collective-permute-done | bytes 262176 | tf_op jit(solution)/shard_map/ppermute | solution.py:21
  22.9 0.1 fusion.12
  23.1 1.3 collective-permute-start.2
  24.4 1.3 collective-permute-start.3
  26.4 1.7 multiply_convert_fusion
  28.1 0.0 collective-permute-done.2
  28.1 1.6 collective-permute-done.3
  29.7 1.6 pad_maximum_fusion.ext_ref
  31.3 14.5 %frames.1 = (f32[2,7,768,128]{3,2,1,0:T(8,128)}, f32[2048,128]{1,0:T(8,128)}) custom-call(s32[1]{0:T(128)} %bitcast.14.count_ref, s32[2,8]{1,0:T(2,128)} %bitcast.20, bf16[2,768,768]{2,1,0:T(8,128)(2,1)} %pad_maximum_fusion.ext_ref, f32[2,2,256,256]{3,2,1,0:T(8,128)} %probe_ref.1, bf16[8,256,256]{2,1,0:T(8,128)(2,1)} %bitcast.19, ...), custom_call_target="tpu_custom_call" | custom-call | tf_op jit(solution)/shard_map/frames/pallas_call | solution.py:179
  45.8 4.8 %slice_bitcast_fusion = f32[2,768,6,128]{3,1,2,0:T(8,128)} fusion(f32[2,7,768,128]{3,2,1,0:T(8,128)} %get-tuple-element.52), kind=kLoop, calls=%fused_computation | loop fusion | bytes 9437184 | tf_op jit(solution)/shard_map/transpose | solution.py:215
  50.6 6.1 %copy.8 = f32[2,768,6,128]{1,3,2,0:T(8,128)} copy(f32[2,768,6,128]{3,1,2,0:T(8,128)} %slice_bitcast_fusion) | data formatting | bytes 9437184 | tf_op jit(solution)/shard_map/transpose | solution.py:215
  56.7 0.0 copy-start
  56.7 2.7 %bitcast_convert_fusion = bf16[2,768,768]{1,2,0:T(8,128)(2,1)S(1)} fusion(f32[2,768,6,128]{1,3,2,0:T(8,128)} %copy.8), kind=kLoop, calls=%fused_computation.26 | loop fusion | flops 1179648 | bytes 7077888 | tf_op jit(solution)/shard_map/convert.3
  59.4 0.9 fusion.10
  60.2 4.2 %collective-permute-start.4 = (bf16[2,128,768]{1,2,0:T(8,128)(2,1)}, bf16[2,128,768]{1,2,0:T(8,128)(2,1)}, u32[]{:S(2)}, u32[]{:S(2)}) collective-permute-start(bf16[2,128,768]{1,2,0:T(8,128)(2,1)} %get-tuple-element.57), channel_id=1, source_target_pairs={{0,8},{8,16},{16,24},{1,9},{9,17},{17,25},{2,10},{10,18},{18,26},{... | collective-permute-start | bytes 1179656 | tf_op jit(solution)/shard_map/ppermute | solution.py:29
  64.4 1.3 collective-permute-start.5
  65.7 0.0 copy-done
  65.7 1.1 copy.13
  66.8 0.0 all-reduce.2.cloned.1.call-update
  66.8 2.2 slice.152
  69.0 0.3 collective-permute-done.4
  69.3 1.4 fusion.1
  70.7 6.6 %collective-permute-done.5 = bf16[2,128,768]{1,2,0:T(8,128)(2,1)} collective-permute-done((bf16[2,128,768]{1,2,0:T(8,128)(2,1)S(1)}, bf16[2,128,768]{1,2,0:T(8,128)(2,1)}, u32[]{:S(2)}, u32[]{:S(2)}) %collective-permute-start.5) | collective-permute-done | bytes 393248 | tf_op jit(solution)/shard_map/ppermute | solution.py:29
  77.3 1.2 fusion
  78.4 0.2 convert.9
  78.7 1.5 slice.157
  80.2 0.8 fusion.11
  81.0 1.3 collective-permute-start.7
  82.3 9.5 %collective-permute-start.6 = (bf16[2,512,128]{1,2,0:T(8,128)(2,1)}, bf16[2,512,128]{1,2,0:T(8,128)(2,1)}, u32[]{:S(2)}, u32[]{:S(2)}) collective-permute-start(bf16[2,512,128]{1,2,0:T(8,128)(2,1)} %get-tuple-element.59), channel_id=1, source_target_pairs={{0,1},{1,2},{2,3},{3,4},{4,5},{5,6},{6,7},{8,9},{9,10},{10,11},{11... | collective-permute-start | bytes 786440 | tf_op jit(solution)/shard_map/ppermute | solution.py:29
  91.8 121.0 %all-reduce.2.cloned.1.call-done = f32[2,2,256,256]{3,2,1,0:T(8,128)} async-done(((f32[2,2,256,256]{3,2,1,0:T(8,128)}), f32[2,2,256,256]{3,2,1,0:T(8,128)}) %all-reduce.2.cloned.1.call-update) | async-done | bytes 1048592 | tf_op jit(solution)/shard_map/psum | solution.py:238
  212.8 2.3 broadcast_multiply_fusion
  215.1 0.0 collective-permute-done.6
  215.1 1.8 fusion.3
  216.9 0.0 collective-permute-done.7
  216.9 1.9 fusion.2
  218.8 2.9 %copy.10 = f32[2,512,512]{2,1,0:T(8,128)} copy(f32[2,512,512]{1,2,0:T(8,128)} %fusion.2) | data formatting | bytes 4194304
  (2 shorter events, 0.0 us)
Async XLA Ops:
  7.2 205.6 %all-reduce.2.cloned.1.call-start = ((), (), s32[]{:S(2)}) async-start(), calls=%async_computation | async-start | bytes 2097152 | tf_op jit(solution)/shard_map/psum | solution.py:238
  8.3 10.5 %collective-permute-start = (bf16[2,128,512]{2,1,0:T(8,128)(2,1)S(1)}, bf16[2,128,512]{2,1,0:T(8,128)(2,1)S(1)}, u32[]{:S(2)}, u32[]{:S(2)}) collective-permute-start(bf16[2,128,512]{2,1,0:T(8,128)(2,1)S(1)} %get-tuple-element.63), channel_id=1, source_target_pairs={{0,8},{8,16},{16,24},{1,9},{9,17},{17,25},{2,10},{10,18},{18,26},{... | collective-permute-start | bytes 786440 | tf_op jit(solution)/shard_map/ppermute | solution.py:20
  13.3 9.7 %collective-permute-start.1 = (bf16[2,128,512]{2,1,0:T(8,128)(2,1)S(1)}, bf16[2,128,512]{2,1,0:T(8,128)(2,1)S(1)}, u32[]{:S(2)}, u32[]{:S(2)}) collective-permute-start(bf16[2,128,512]{2,1,0:T(8,128)(2,1)S(1)} %get-tuple-element.62), channel_id=1, source_target_pairs={{8,0},{16,8},{24,16},{9,1},{17,9},{25,17},{10,2},{18,10},{26,18},{... | collective-permute-start | bytes 786440 | tf_op jit(solution)/shard_map/ppermute | solution.py:21
  23.1 5.0 %collective-permute-start.2 = (bf16[2,768,128]{2,1,0:T(8,128)(2,1)S(1)}, bf16[2,768,128]{2,1,0:T(8,128)(2,1)S(1)}, u32[]{:S(2)}, u32[]{:S(2)}) collective-permute-start(bf16[2,768,128]{2,1,0:T(8,128)(2,1)S(1)} %get-tuple-element.60), channel_id=1, source_target_pairs={{0,1},{1,2},{2,3},{3,4},{4,5},{5,6},{6,7},{8,9},{9,10},{10,11},{11... | collective-permute-start | bytes 1179656 | tf_op jit(solution)/shard_map/ppermute | solution.py:20
  24.4 5.3 %collective-permute-start.3 = (bf16[2,768,128]{2,1,0:T(8,128)(2,1)S(1)}, bf16[2,768,128]{2,1,0:T(8,128)(2,1)S(1)}, u32[]{:S(2)}, u32[]{:S(2)}) collective-permute-start(bf16[2,768,128]{2,1,0:T(8,128)(2,1)S(1)} %get-tuple-element.61), channel_id=1, source_target_pairs={{1,0},{2,1},{3,2},{4,3},{5,4},{6,5},{7,6},{9,8},{10,9},{11,10},{12... | collective-permute-start | bytes 1179656 | tf_op jit(solution)/shard_map/ppermute | solution.py:21
  56.7 9.0 %copy-start = (f32[2048,128]{1,0:T(8,128)S(1)}, f32[2048,128]{1,0:T(8,128)}, u32[]{:S(2)}) copy-start(f32[2048,128]{1,0:T(8,128)} %get-tuple-element.53) | copy-start | bytes 3145732
  60.2 9.1 %collective-permute-start.4 = (bf16[2,128,768]{1,2,0:T(8,128)(2,1)}, bf16[2,128,768]{1,2,0:T(8,128)(2,1)}, u32[]{:S(2)}, u32[]{:S(2)}) collective-permute-start(bf16[2,128,768]{1,2,0:T(8,128)(2,1)} %get-tuple-element.57), channel_id=1, source_target_pairs={{0,8},{8,16},{16,24},{1,9},{9,17},{17,25},{2,10},{10,18},{18,26},{... | collective-permute-start | bytes 1179656 | tf_op jit(solution)/shard_map/ppermute | solution.py:29
  64.4 12.8 %collective-permute-start.5 = (bf16[2,128,768]{1,2,0:T(8,128)(2,1)S(1)}, bf16[2,128,768]{1,2,0:T(8,128)(2,1)}, u32[]{:S(2)}, u32[]{:S(2)}) collective-permute-start(bf16[2,128,768]{1,2,0:T(8,128)(2,1)S(1)} %get-tuple-element.56), channel_id=1, source_target_pairs={{8,0},{16,8},{24,16},{9,1},{17,9},{25,17},{10,2},{18,10},{26,18},{... | collective-permute-start | bytes 1179656 | tf_op jit(solution)/shard_map/ppermute | solution.py:29
  81.0 135.9 %collective-permute-start.7 = (bf16[2,512,128]{1,2,0:T(8,128)(2,1)}, bf16[2,512,128]{1,2,0:T(8,128)(2,1)S(1)}, u32[]{:S(2)}, u32[]{:S(2)}) collective-permute-start(bf16[2,512,128]{1,2,0:T(8,128)(2,1)} %get-tuple-element.58), channel_id=1, source_target_pairs={{1,0},{2,1},{3,2},{4,3},{5,4},{6,5},{7,6},{9,8},{10,9},{11,10},{12... | collective-permute-start | bytes 786440 | tf_op jit(solution)/shard_map/ppermute | solution.py:29
  82.3 132.8 %collective-permute-start.6 = (bf16[2,512,128]{1,2,0:T(8,128)(2,1)}, bf16[2,512,128]{1,2,0:T(8,128)(2,1)}, u32[]{:S(2)}, u32[]{:S(2)}) collective-permute-start(bf16[2,512,128]{1,2,0:T(8,128)(2,1)} %get-tuple-element.59), channel_id=1, source_target_pairs={{0,1},{1,2},{2,3},{3,4},{4,5},{5,6},{6,7},{8,9},{9,10},{10,11},{11... | collective-permute-start | bytes 786440 | tf_op jit(solution)/shard_map/ppermute | solution.py:29
Sparse Core Ops, SparseCore 0:
  66.9 145.7 all-reduce.1

commit v2 on v1

--- a/solution.py
+++ b/solution.py
@@ -1,46 +1,362 @@
+import functools
 import math
 
 import jax
 import jax.numpy as jnp
+import numpy as np
 from jax import lax
 from jax.experimental import pallas as pl
 from jax.experimental.pallas import tpu as pltpu
 from jax.sharding import PartitionSpec as P
 
 HALO = 128
-
-
-def with_halo(value, sides, width):
-    for axis, dim in sides:
-        devices, length = (lax.axis_size(axis), value.shape[dim])
-        up = [(i, (i + 1) % devices) for i in range(devices - 1)]
-        down = [(j, i) for i, j in up]
-        last = lax.slice_in_dim(value, length - width, length, axis=dim)
-        leading = lax.slice_in_dim(value, 0, width, axis=dim)
-        before = lax.ppermute(last, axis, up)
-        after = lax.ppermute(leading, axis, down)
-        value = jnp.concatenate([before, value, after], axis=dim)
-    return value
-
-
-def from_behind(value, axis, by):
-    devices = lax.axis_size(axis)
-    pairs = [(i, i + by) for i in range(devices) if 0 <= i + by < devices]
-    return lax.ppermute(value, axis, pairs)
+LANES = 128
+
+
+MESH = pl.DeviceIdType.MESH
+SIDES = [(dr, dc) for dr in (-1, 0, 1) for dc in (-1, 0, 1) if (dr, dc) != (0, 0)]
+
+
+def position():
+    return (
+        lax.axis_index("row"),
+        lax.axis_index("col"),
+        lax.axis_size("row"),
+        lax.axis_size("col"),
+    )
+
+
+def exists(side):
+    row, col, rows, cols = position()
+    dr, dc = side
+    inside = jnp.bool_(True)
+    if dr:
+        inside = row + dr >= 0 if dr < 0 else row + dr < rows
+    if dc:
+        other = col + dc >= 0 if dc < 0 else col + dc < cols
+        inside = jnp.logical_and(inside, other) if dr else other
+    return inside
+
+
+def at_side(side):
+    row, col, _, _ = position()
+    return (row + side[0], col + side[1])
+
+
+def opposite(side):
+    return (-side[0], -side[1])
+
+
+def part(step, margin, inner):
+    return {-1: slice(0, margin), 0: slice(margin, margin + inner), 1: slice(margin + inner, None)}[
+        step
+    ]
+
+
+def edge(step, margin, inner):
+    return {-1: slice(0, margin), 0: slice(0, inner), 1: slice(inner - margin, inner)}[step]
+
+
+def to_side(side, index, source, landing, send_sems, recv_sems):
+    return pltpu.make_async_remote_copy(
+        src_ref=source,
+        dst_ref=landing,
+        send_sem=send_sems.at[index],
+        recv_sem=recv_sems.at[index],
+        device_id=at_side(side),
+        device_id_type=MESH,
+    )
+
+
+def halo_kernel(object_ref, ext_ref, *scratch):
+    landings, (send_sems, recv_sems) = scratch[: len(SIDES)], scratch[len(SIDES) :]
+    side_rows, side_cols = object_ref.shape[1:]
+    barrier = pltpu.get_barrier_semaphore()
+    count = jnp.int32(0)
+    for side in SIDES:
+
+        @pl.when(exists(side))
+        def _(side=side):
+            pl.semaphore_signal(barrier, inc=1, device_id=at_side(side), device_id_type=MESH)
+
+        count = count + exists(side).astype(jnp.int32)
+    pl.semaphore_wait(barrier, count)
+
+    def copy(index):
+        dr, dc = SIDES[index]
+        source = object_ref.at[:, edge(dr, HALO, side_rows), edge(dc, HALO, side_cols)]
+        return to_side(SIDES[index], index, source, landings[index], send_sems, recv_sems)
+
+    for index, side in enumerate(SIDES):
+
+        @pl.when(exists(side))
+        def _(index=index):
+            copy(index).start()
+
+    for t in range(side_cols // LANES):
+        ext_ref[:, HALO // LANES + t, HALO : HALO + side_rows, :] = object_ref[
+            :, :, t * LANES : (t + 1) * LANES
+        ]
+    for index, side in enumerate(SIDES):
+        dr, dc = opposite(side)
+        rows = part(dr, HALO, side_rows)
+        tiles = range(ext_ref.shape[1])[part(dc, HALO // LANES, side_cols // LANES)]
+
+        @pl.when(exists((dr, dc)))
+        def _(index=index, rows=rows, tiles=tiles):
+            copy(index).wait_recv()
+            for k, t in enumerate(tiles):
+                ext_ref[:, t, rows, :] = landings[index][:, :, k * LANES : (k + 1) * LANES]
+
+        @pl.when(jnp.logical_not(exists((dr, dc))))
+        def _(rows=rows, tiles=tiles, index=index):
+            for t in tiles:
+                ext_ref[:, t, rows, :] = jnp.zeros(
+                    (2, landings[index].shape[1], LANES), ext_ref.dtype
+                )
+
+    for index, side in enumerate(SIDES):
+
+        @pl.when(exists(side))
+        def _(index=index):
+            copy(index).wait_send()
+
+
+def halo_call(object_field):
+    _, side_rows, side_cols = object_field.shape
+    vmem = pl.BlockSpec(memory_space=pltpu.VMEM)
+    landings = []
+    for dr, dc in SIDES:
+        landings.append(
+            pltpu.VMEM((2, HALO if dr else side_rows, HALO if dc else side_cols), object_field.dtype)
+        )
+    sems = pltpu.SemaphoreType.DMA((len(SIDES),))
+    return pl.pallas_call(
+        halo_kernel,
+        out_shape=jax.ShapeDtypeStruct(
+            (2, (side_cols + 2 * HALO) // LANES, side_rows + 2 * HALO, LANES), object_field.dtype
+        ),
+        in_specs=[vmem],
+        out_specs=vmem,
+        scratch_shapes=landings + [sems, sems],
+        compiler_params=pltpu.CompilerParams(
+            collective_id=0, has_side_effects=True, vmem_limit_bytes=32 * 1024 * 1024
+        ),
+        name="halo",
+    )(object_field)
+
+
+def reduce_kernel(scale, acc_ref, pacc_ref, grad_ref, probe_ref, *scratch):
+    count = len(SIDES)
+    sends, landings, rest = scratch[:count], scratch[count : 2 * count], scratch[2 * count :]
+    psend, precv, zsend, zrecv, full, side_sems, col_sems, row_sems = rest
+    row, col, n_row, n_col = position()
+    side_rows, side_cols = grad_ref.shape[1:]
+    margin = HALO // LANES
+    inner = side_cols // LANES
+    for index, (dr, dc) in enumerate(SIDES):
+        tiles = range(inner + 2 * margin)[part(dc, margin, inner)]
+        rows = part(dr, HALO, side_rows)
+        for k, t in enumerate(tiles):
+            sends[index][:, k] = acc_ref[:, t, rows, :].astype(jnp.bfloat16)
+    psend[...] = pacc_ref[...].astype(jnp.bfloat16)
+
+    barrier = pltpu.get_barrier_semaphore()
+    waits = jnp.int32(n_row + n_col - 2)
+    for k in range(1, n_col):
+        pl.semaphore_signal(
+            barrier, inc=1, device_id=(row, lax.rem(col + k, n_col)), device_id_type=MESH
+        )
+    for k in range(1, n_row):
+        pl.semaphore_signal(
+            barrier, inc=1, device_id=(lax.rem(row + k, n_row), col), device_id_type=MESH
+        )
+    for side in SIDES:
+        if side[0] and side[1]:
+
+            @pl.when(exists(side))
+            def _(side=side):
+                pl.semaphore_signal(barrier, inc=1, device_id=at_side(side), device_id_type=MESH)
+
+            waits = waits + exists(side).astype(jnp.int32)
+    pl.semaphore_wait(barrier, waits)
+
+    share = psend.shape[0] // n_col
+    piece = share // n_row
+
+    def to_peer(source, landing, sems, which, k, device):
+        return pltpu.make_async_remote_copy(
+            src_ref=source,
+            dst_ref=landing,
+            send_sem=sems.at[which, k - 1],
+            recv_sem=sems.at[which + 1, k - 1],
+            device_id=device,
+            device_id_type=MESH,
+        )
+
+    def col_peer(k):
+        return (row, lax.rem(col + k, n_col))
+
+    def row_peer(k):
+        return (lax.rem(row + k, n_row), col)
+
+    def share_of(ref, index):
+        return ref.at[pl.ds(pl.multiple_of(index * share, share), share)]
+
+    def scatter_copy(k):
+        return to_peer(
+            share_of(psend, lax.rem(col + k, n_col)), precv.at[k - 1], col_sems, 0, k, col_peer(k)
+        )
+
+    def row_scatter_copy(k):
+        target = lax.rem(row + k, n_row)
+        return to_peer(
+            zsend.at[pl.ds(pl.multiple_of(target * piece, piece), piece)],
+            zrecv.at[k - 1],
+            row_sems,
+            0,
+            k,
+            row_peer(k),
+        )
+
+    def piece_of(index):
+        start = pl.multiple_of(col * share + index * piece, piece)
+        return full.at[pl.ds(start, piece)]
+
+    def row_gather_copy(k, owner):
+        return to_peer(piece_of(row), piece_of(owner), row_sems, 2, k, row_peer(k))
+
+    def gather_copy(k, owner):
+        return to_peer(share_of(full, col), share_of(full, owner), col_sems, 2, k, col_peer(k))
+
+    def side_copy(index):
+        return to_side(
+            SIDES[index], index, sends[index], landings[index], side_sems.at[0], side_sems.at[1]
+        )
+
+    for k in range(1, n_col):
+        scatter_copy(k).start()
+    for index, side in enumerate(SIDES):
+
+        @pl.when(exists(side))
+        def _(index=index):
+            side_copy(index).start()
+
+    for t in range(inner):
+        grad_ref[:, :, t * LANES : (t + 1) * LANES] = acc_ref[
+            :, margin + t, HALO : HALO + side_rows, :
+        ]
+    total = pacc_ref[pl.ds(pl.multiple_of(col * share, share), share), :]
+    for k in range(1, n_col):
+        scatter_copy(k).wait_recv()
+        total = total + precv[k - 1].astype(jnp.float32)
+    zsend[...] = total
+    for k in range(1, n_row):
+        row_scatter_copy(k).start()
+    own = zsend[pl.ds(pl.multiple_of(row * piece, piece), piece), :]
+    for k in range(1, n_row):
+        row_scatter_copy(k).wait_recv()
+        own = own + zrecv[k - 1]
+    start = pl.multiple_of(col * share + row * piece, piece)
+    full[pl.ds(start, piece), :] = (own * scale).astype(jnp.bfloat16)
+    for k in range(1, n_row):
+        row_gather_copy(k, row).start()
+    for k in range(1, n_row):
+        row_gather_copy(k, lax.rem(row + n_row - k, n_row)).wait_recv()
+    for k in range(1, n_col):
+        gather_copy(k, col).start()
+
+    for index, side in enumerate(SIDES):
+        dr, dc = opposite(side)
+        rows = edge(dr, HALO, side_rows)
+        tiles = range(inner)[edge(dc, margin, inner)]
+
+        @pl.when(exists((dr, dc)))
+        def _(index=index, rows=rows, tiles=tiles):
+            side_copy(index).wait_recv()
+            for k, t in enumerate(tiles):
+                grad_ref[:, rows, t * LANES : (t + 1) * LANES] += landings[index][:, k].astype(
+                    jnp.float32
+                )
+
+    for k in range(1, n_col):
+        gather_copy(k, lax.rem(col + n_col - k, n_col)).wait_recv()
+    parts, modes, fs, width = probe_ref.shape
+    at = 0
+    for p in range(parts):
+        for m in range(modes):
+            for t in range(width // LANES):
+                probe_ref[p, m, :, t * LANES : (t + 1) * LANES] = full[at : at + fs, :].astype(
+                    jnp.float32
+                )
+                at += fs
+    for k in range(1, n_col):
+        scatter_copy(k).wait_send()
+        gather_copy(k, col).wait_send()
+    for k in range(1, n_row):
+        row_scatter_copy(k).wait_send()
+        row_gather_copy(k, row).wait_send()
+    for index, side in enumerate(SIDES):
+
+        @pl.when(exists(side))
+        def _(index=index):
+            side_copy(index).wait_send()
+
+
+def reduce_call(acc, probe_flat, object_shape, probe_shape, scale):
+    n_row, n_col = lax.axis_size("row"), lax.axis_size("col")
+    _, side_rows, side_cols = object_shape
+    inner = side_cols // LANES
+    margin = HALO // LANES
+    vmem = pl.BlockSpec(memory_space=pltpu.VMEM)
+    buffers = []
+    for dr, dc in SIDES:
+        buffers.append(
+            pltpu.VMEM(
+                (2, margin if dc else inner, HALO if dr else side_rows, LANES), jnp.bfloat16
+            )
+        )
+    total_rows = probe_flat.shape[0]
+    share = total_rows // n_col
+    piece = share // n_row
+    return pl.pallas_call(
+        functools.partial(reduce_kernel, scale),
+        out_shape=(
+            jax.ShapeDtypeStruct(object_shape, jnp.float32),
+            jax.ShapeDtypeStruct(probe_shape, jnp.float32),
+        ),
+        in_specs=[vmem, vmem],
+        out_specs=(vmem, vmem),
+        scratch_shapes=buffers
+        + buffers
+        + [
+            pltpu.VMEM((total_rows, LANES), jnp.bfloat16),
+            pltpu.VMEM((n_col - 1, share, LANES), jnp.bfloat16),
+            pltpu.VMEM((share, LANES), jnp.float32),
+            pltpu.VMEM((n_row - 1, piece, LANES), jnp.float32),
+            pltpu.VMEM((total_rows, LANES), jnp.bfloat16),
+            pltpu.SemaphoreType.DMA((2, len(SIDES))),
+            pltpu.SemaphoreType.DMA((4, n_col - 1)),
+            pltpu.SemaphoreType.DMA((4, n_row - 1)),
+        ],
+        compiler_params=pltpu.CompilerParams(
+            collective_id=1, has_side_effects=True, vmem_limit_bytes=48 * 1024 * 1024
+        ),
+        name="reduce",
+    )(acc, probe_flat)
 
 
 def fourier_tables(frame_side):
-    indices = jnp.arange(frame_side, dtype=jnp.int32)
+    indices = np.arange(frame_side)
     product = indices[:, None] * indices[None, :] % frame_side
-    angles = 2.0 * math.pi / frame_side * product.astype(jnp.float32)
+    angles = 2.0 * math.pi / frame_side * product
     norm_scale = 1.0 / math.sqrt(frame_side)
     return (
-        (jnp.cos(angles) * norm_scale).astype(jnp.bfloat16),
-        (-jnp.sin(angles) * norm_scale).astype(jnp.bfloat16),
+        jnp.asarray((np.cos(angles) * norm_scale).astype(np.float32)).astype(jnp.bfloat16),
+        jnp.asarray((-np.sin(angles) * norm_scale).astype(np.float32)).astype(jnp.bfloat16),
     )
 
 
-LANES = 128
 CHUNK = 32
 
 
@@ -54,11 +370,11 @@
 ):
     fs = probe_ref.shape[-1]
     modes = probe_ref.shape[1]
-    tiles = ext_ref.shape[2] // LANES
+    tiles = ext_ref.shape[1]
     lane_tiles = fs // LANES
     for plane in range(2):
         for t in range(tiles):
-            extf[plane, t] = ext_ref[plane, :, t * LANES : (t + 1) * LANES].astype(jnp.float32)
+            extf[plane, t] = ext_ref[plane, t].astype(jnp.float32)
         extf[plane, tiles] = jnp.zeros(extf.shape[2:], jnp.float32)
     acc_ref[...] = jnp.zeros(acc_ref.shape, jnp.float32)
     pacc_ref[...] = jnp.zeros(pacc_ref.shape, jnp.float32)
@@ -172,8 +488,7 @@
 def frames_call(extended, probe_modes, amplitudes, positions, live_count, tables):
     fs = probe_modes.shape[-1]
     modes = probe_modes.shape[1]
-    ext_rows, ext_cols = extended.shape[1:]
-    tiled = (2, ext_cols // LANES + 1, ext_rows, LANES)
+    tiled = (2, extended.shape[1] + 1, extended.shape[2], LANES)
     vmem = pl.BlockSpec(memory_space=pltpu.VMEM)
     smem = pl.BlockSpec(memory_space=pltpu.SMEM)
     return pl.pallas_call(
@@ -199,45 +514,18 @@
 
 
 def shards(object_field, probe_modes, measured_amp, scan_positions, frame_counts):
-    frame_side = probe_modes.shape[-1]
     slot_count = measured_amp.shape[2]
-    tile_side = object_field.shape[1]
-    extended = with_halo(object_field, (("row", 1), ("col", 2)), HALO)
-    amplitudes = measured_amp[0, 0]
+    extended = halo_call(object_field)
     acc, probe_flat = frames_call(
         extended,
         probe_modes,
-        amplitudes,
+        measured_amp[0, 0],
         scan_positions[0, 0],
         frame_counts[0, 0],
-        fourier_tables(frame_side),
+        fourier_tables(probe_modes.shape[-1]),
     )
-    gradient = acc[:, :-1].transpose(0, 2, 1, 3).reshape(extended.shape)
-    modes = probe_modes.shape[1]
-    probe_local = probe_flat.reshape(2, modes, frame_side // LANES, frame_side, LANES)
-    probe_local = probe_local.transpose(0, 1, 3, 2, 4).reshape(probe_modes.shape)
-    low_end = tile_side + HALO
-    from_above = from_behind(gradient[:, low_end:, :].astype(jnp.bfloat16), "row", 1).astype(
-        jnp.float32
-    )
-    from_below = from_behind(gradient[:, :HALO, :].astype(jnp.bfloat16), "row", -1).astype(
-        jnp.float32
-    )
-    middle = gradient[:, HALO:low_end, :]
-    middle = middle.at[:, :HALO, :].add(from_above)
-    middle = middle.at[:, tile_side - HALO :, :].add(from_below)
-    from_left = from_behind(middle[:, :, low_end:].astype(jnp.bfloat16), "col", 1).astype(
-        jnp.float32
-    )
-    from_right = from_behind(middle[:, :, :HALO].astype(jnp.bfloat16), "col", -1).astype(
-        jnp.float32
-    )
-    interior = middle[:, :, HALO:low_end]
-    interior = interior.at[:, :, :HALO].add(from_left)
-    interior = interior.at[:, :, tile_side - HALO :].add(from_right)
-    probe_total = lax.psum(probe_local, ("row", "col"))
     norm_scale = 1.0 / math.sqrt(lax.axis_size("row") * lax.axis_size("col") * slot_count)
-    return (interior, probe_total * norm_scale)
+    return reduce_call(acc, probe_flat, object_field.shape, probe_modes.shape, norm_scale)
 
 
 def solution(mesh):

time: 229 us -> 76 us (0.33)
  waiting for transfers between devices: 137 us -> 0 us
  Pallas kernels: 14.5 us -> 69.4 us
  starting transfers between devices: 25.2 us -> 0 us
  local copies, waits for them, and re-layouts: 22.8 us -> 6.13 us
  other arithmetic: 14.8 us -> 0 us
  between operations: 14.8 us -> 1.31 us
    psum x1 -> x0, waiting for transfers between devices: 121 us -> none  [shards(): probe_total = lax.psum(probe_local, ('row', 'col'))]
    pallas_call x0 -> x2, Pallas kernels: none -> 57.1 us  [the longest x1 45.4 us: reduce_call(): pl.pallas_call(functools.partial(reduce_kernel, scale), out_shape=(jax.Sh...]
    ppermute x8 -> x0, starting transfers between devices: 25.2 us -> none  [the longest x4 16.3 us: from_behind(): return lax.ppermute(value, axis, pairs)]
    ppermute x8 -> x0, waiting for transfers between devices: 15.6 us -> none  [the longest x4 6.89 us: from_behind(): return lax.ppermute(value, axis, pairs)]
    transpose x2 -> x0, local copies, waits for them, and re-layouts: 10.9 us -> none  [shards(): gradient = acc[:, :-1].transpose(0, 2, 1, 3).reshape(extended.shape)]
    slice x6 -> x0, local copies, waits for them, and re-layouts: 6.61 us -> none  [the longest x1 2.2 us: shards(): middle = gradient[:, HALO:low_end, :]]
    scatter-add x4 -> x0, other arithmetic: 6.26 us -> none  [the longest x1 1.92 us: shards(): interior = interior.at[:, :, tile_side - HALO:].add(from_right)]
    another operation x2 -> x0, other arithmetic: 2.86 us -> none
  transfers between devices with their start and end apart: 9 -> 0, of which waited for: 6 -> 0; matrix products, arithmetic and copies ran while one was open for 7% -> 0% of each run, Pallas kernels for 0% -> 0%
where the time goes in v2:
time: 76 us; the launch traced here: 76.9 us
  Pallas kernels  69.4 us (91%)
  local copies, waits for them, and re-layouts  6.13 us (8%)
  between operations  1.31 us (2%)
    pallas_call x1, Pallas kernels, reduce_call(): pl.pallas_call(functools.partial(reduce_kernel, scale), out_shape=(jax.Sh...  45.4 us
    pallas_call x1, Pallas kernels, frames_call(): pl.pallas_call(frames_kernel, out_shape=(jax.ShapeDtypeStruct(tiled, jnp....  12.3 us
    pallas_call x1, Pallas kernels, halo_call(): pl.pallas_call(halo_kernel, out_shape=jax.ShapeDtypeStruct((2, (side_cols...  11.8 us
    unnamed x8, local copies, waits for them, and re-layouts  6.13 us

profile of v2, /device:TPU:0, one launch (start us, length us, event | category | flops | bytes accessed | tf_op | source)
XLA Modules:
  0.0 76.9 jit_solution(17229869240747852584)
XLA Ops:
  1.3 0.0 copy-start.2
  1.3 1.2 %copy-done.2 = bf16[2,512,512]{2,1,0:T(8,128)(2,1)S(1)} copy-done((bf16[2,512,512]{2,1,0:T(8,128)(2,1)S(1)}, bf16[2,512,512]{2,1,0:T(8,128)(2,1)}, u32[]{:S(2)}) %copy-start.2) | copy-done | bytes 1048600
  2.5 11.8 %halo.1.ext_ref = bf16[2,6,768,128]{3,2,1,0:T(8,128)(2,1)S(1)} custom-call(bf16[2,512,512]{2,1,0:T(8,128)(2,1)S(1)} %copy-done.2), custom_call_target="tpu_custom_call" | custom-call | tf_op jit(solution)/shard_map/halo/pallas_call | solution.py:134
  14.3 0.0 copy-start
  14.3 1.4 %copy-done = bf16[2,6,768,128]{3,2,1,0:T(8,128)(2,1)} copy-done((bf16[2,6,768,128]{3,2,1,0:T(8,128)(2,1)}, bf16[2,6,768,128]{3,2,1,0:T(8,128)(2,1)S(1)}, u32[]{:S(2)}) %copy-start) | copy-done | bytes 2359320
  15.7 12.3 %frames.1 = (f32[2,7,768,128]{3,2,1,0:T(8,128)}, f32[2048,128]{1,0:T(8,128)}) custom-call(s32[1]{0:T(128)} %bitcast.3.count_ref, s32[2,8]{1,0:T(2,128)} %bitcast.5, bf16[2,6,768,128]{3,2,1,0:T(8,128)(2,1)} %copy-done, f32[2,2,256,256]{3,2,1,0:T(8,128)} %probe_ref.1, bf16[8,256,256]{2,1,0:T(8,128)(2,1)} %bitcast.4, bf16[256,256]{1,0:T(8,128)(2,1)} %constant.9.tr_ref, ...), custom_call_target="tpu_custom_call" | custom-call | tf_op jit(solution)/shard_map/frames/pallas_call | solution.py:494
  28.0 0.0 copy-start.1
  28.0 1.2 %copy-done.1 = f32[2048,128]{1,0:T(8,128)S(1)} copy-done((f32[2048,128]{1,0:T(8,128)S(1)}, f32[2048,128]{1,0:T(8,128)}, u32[]{:S(2)}) %copy-start.1) | copy-done | bytes 1048600
  29.2 45.4 %reduce.1 = (f32[2,512,512]{2,1,0:T(8,128)S(1)}, f32[2,2,256,256]{3,2,1,0:T(8,128)S(1)}) custom-call(f32[2,7,768,128]{3,2,1,0:T(8,128)} %get-tuple-element.4.acc_ref, f32[2048,128]{1,0:T(8,128)S(1)} %copy-done.1), custom_call_target="tpu_custom_call" | custom-call | tf_op jit(solution)/shard_map/reduce/pallas_call | solution.py:322
  74.6 1.3 %copy.12 = f32[2,512,512]{2,1,0:T(8,128)} copy(f32[2,512,512]{2,1,0:T(8,128)S(1)} %get-tuple-element.8) | data formatting | bytes 4194304
  75.9 1.0 %copy.13 = f32[2,2,256,256]{3,2,1,0:T(8,128)} copy(f32[2,2,256,256]{3,2,1,0:T(8,128)S(1)} %get-tuple-element.9) | data formatting | bytes 2097152
Async XLA Ops:
  1.3 1.2 %copy-start.2 = (bf16[2,512,512]{2,1,0:T(8,128)(2,1)S(1)}, bf16[2,512,512]{2,1,0:T(8,128)(2,1)}, u32[]{:S(2)}) copy-start(bf16[2,512,512]{2,1,0:T(8,128)(2,1)} %object_ref.1) | copy-start | bytes 3145732
  14.3 1.4 %copy-start = (bf16[2,6,768,128]{3,2,1,0:T(8,128)(2,1)}, bf16[2,6,768,128]{3,2,1,0:T(8,128)(2,1)S(1)}, u32[]{:S(2)}) copy-start(bf16[2,6,768,128]{3,2,1,0:T(8,128)(2,1)S(1)} %halo.1.ext_ref) | copy-start | bytes 7077892
  28.0 1.2 %copy-start.1 = (f32[2048,128]{1,0:T(8,128)S(1)}, f32[2048,128]{1,0:T(8,128)}, u32[]{:S(2)}) copy-start(f32[2048,128]{1,0:T(8,128)} %get-tuple-element.5.pacc_ref) | copy-start | bytes 3145732

commit v3 on v2

--- a/solution.py
+++ b/solution.py
@@ -140,7 +140,7 @@
         out_specs=vmem,
         scratch_shapes=landings + [sems, sems],
         compiler_params=pltpu.CompilerParams(
-            collective_id=0, has_side_effects=True, vmem_limit_bytes=32 * 1024 * 1024
+            collective_id=0, has_side_effects=True, vmem_limit_bytes=10 * 1024 * 1024
         ),
         name="halo",
     )(object_field)
@@ -236,12 +236,16 @@
 
     for k in range(1, n_col):
         scatter_copy(k).start()
-    for index, side in enumerate(SIDES):
-
-        @pl.when(exists(side))
-        def _(index=index):
-            side_copy(index).start()
-
+
+    def start_sides(chosen):
+        for index, side in enumerate(SIDES):
+            if chosen(side):
+
+                @pl.when(exists(side))
+                def _(index=index):
+                    side_copy(index).start()
+
+    start_sides(lambda side: side[1] == 0)
     for t in range(inner):
         grad_ref[:, :, t * LANES : (t + 1) * LANES] = acc_ref[
             :, margin + t, HALO : HALO + side_rows, :
@@ -253,6 +257,8 @@
     zsend[...] = total
     for k in range(1, n_row):
         row_scatter_copy(k).start()
+    start_sides(lambda side: side[0] == 0)
+    start_sides(lambda side: side[0] != 0 and side[1] != 0)
     own = zsend[pl.ds(pl.multiple_of(row * piece, piece), piece), :]
     for k in range(1, n_row):
         row_scatter_copy(k).wait_recv()
@@ -340,7 +346,7 @@
             pltpu.SemaphoreType.DMA((4, n_row - 1)),
         ],
         compiler_params=pltpu.CompilerParams(
-            collective_id=1, has_side_effects=True, vmem_limit_bytes=48 * 1024 * 1024
+            collective_id=1, has_side_effects=True, vmem_limit_bytes=20 * 1024 * 1024
         ),
         name="reduce",
     )(acc, probe_flat)
@@ -508,7 +514,7 @@
             pltpu.VMEM((modes * fs, 2 * fs), jnp.float32),
             pltpu.VMEM((2, fs, fs), jnp.float32),
         ],
-        compiler_params=pltpu.CompilerParams(vmem_limit_bytes=56 * 1024 * 1024),
+        compiler_params=pltpu.CompilerParams(vmem_limit_bytes=26 * 1024 * 1024),
         name="frames",
     )(live_count.reshape(1), positions, extended, probe_modes, amplitudes, *tables)
 

time: 76 us -> 66.3 us (0.87); the launches traced: 76.9 us -> 65.9 us
  Pallas kernels: 69.4 us -> 61 us
  local copies, waits for them, and re-layouts: 6.13 us -> 3.53 us
    pallas_call x1, Pallas kernels: 45.4 us -> 36.9 us  [reduce_call(): pl.pallas_call(functools.partial(reduce_kernel, scale), out_shape=(jax.Sh...]
    unnamed x8 -> x14, local copies, waits for them, and re-layouts: 6.13 us -> 3.53 us
where the time goes in v3:
time: 66.3 us; the launch traced here: 65.9 us
  Pallas kernels  61 us (92%)
  local copies, waits for them, and re-layouts  3.53 us (5%)
  between operations  1.37 us (2%)
    pallas_call x1, Pallas kernels, reduce_call(): pl.pallas_call(functools.partial(reduce_kernel, scale), out_shape=(jax.Sh...  36.9 us
    pallas_call x1, Pallas kernels, frames_call(): pl.pallas_call(frames_kernel, out_shape=(jax.ShapeDtypeStruct(tiled, jnp....  12.4 us
    pallas_call x1, Pallas kernels, halo_call(): pl.pallas_call(halo_kernel, out_shape=jax.ShapeDtypeStruct((2, (side_cols...  11.8 us
    unnamed x14, local copies, waits for them, and re-layouts  3.53 us

profile of v3, /device:TPU:0, one launch (start us, length us, event | category | flops | bytes accessed | tf_op | source)
XLA Modules:
  0.0 65.9 jit_solution(14126873146870005841)
XLA Ops:
  0.6 0.0 copy-start.5
  1.3 0.0 copy-start
  1.3 1.2 %copy-done = bf16[2,512,512]{2,1,0:T(8,128)(2,1)S(1)} copy-done((bf16[2,512,512]{2,1,0:T(8,128)(2,1)S(1)}, bf16[2,512,512]{2,1,0:T(8,128)(2,1)}, u32[]{:S(2)}) %copy-start) | copy-done | bytes 1048600
  2.5 0.0 copy-start.1
  2.5 0.0 copy-start.2
  2.5 0.0 copy-start.3
  2.5 0.0 copy-start.4
  2.5 11.8 %halo.1.ext_ref = bf16[2,6,768,128]{3,2,1,0:T(8,128)(2,1)S(1)} custom-call(bf16[2,512,512]{2,1,0:T(8,128)(2,1)S(1)} %copy-done), custom_call_target="tpu_custom_call" | custom-call | tf_op jit(solution)/shard_map/halo/pallas_call | solution.py:134
  14.3 0.0 copy-done.5
  14.3 0.0 copy-done.1
  14.3 0.0 copy-done.2
  14.4 0.0 copy-done.3
  14.4 0.0 copy-done.4
  14.4 12.4 %frames.1 = (f32[2,7,768,128]{3,2,1,0:T(8,128)S(1)}, f32[2048,128]{1,0:T(8,128)S(1)}) custom-call(s32[1]{0:T(128)} %bitcast.3.count_ref, s32[2,8]{1,0:T(2,128)S(1)} %bitcast.5, bf16[2,6,768,128]{3,2,1,0:T(8,128)(2,1)S(1)} %halo.1.ext_ref, f32[2,2,256,256]{3,2,1,0:T(8,128)S(1)} %copy-done.1, bf16[8,256,256]{2,1,0:T(8,128)(2,1)S(1)} %bitcast.4, ...), custom_call_target="tpu_custom_call" | custom-call | tf_op jit(solution)/shard_map/frames/pallas_call | solution.py:500
  26.8 36.9 %reduce.1 = (f32[2,512,512]{2,1,0:T(8,128)S(1)}, f32[2,2,256,256]{3,2,1,0:T(8,128)S(1)}) custom-call(f32[2,7,768,128]{3,2,1,0:T(8,128)S(1)} %get-tuple-element.4.acc_ref, f32[2048,128]{1,0:T(8,128)S(1)} %get-tuple-element.5.pacc_ref), custom_call_target="tpu_custom_call" | custom-call | tf_op jit(solution)/shard_map/reduce/pallas_call | solution.py:328
  63.6 1.3 %copy.12 = f32[2,512,512]{2,1,0:T(8,128)} copy(f32[2,512,512]{2,1,0:T(8,128)S(1)} %get-tuple-element.8) | data formatting | bytes 4194304
  64.9 1.0 %copy.13 = f32[2,2,256,256]{3,2,1,0:T(8,128)} copy(f32[2,2,256,256]{3,2,1,0:T(8,128)S(1)} %get-tuple-element.9) | data formatting | bytes 2097152
Async XLA Ops:
  0.6 13.7 %copy-start.5 = (s32[1,1,2,8]{3,2,1,0:T(2,128)S(1)}, s32[1,1,2,8]{3,2,1,0:T(2,128)}, u32[]{:S(2)}) copy-start(s32[1,1,2,8]{3,2,1,0:T(2,128)} %param.10) | copy-start | bytes 196
  1.3 1.2 %copy-start = (bf16[2,512,512]{2,1,0:T(8,128)(2,1)S(1)}, bf16[2,512,512]{2,1,0:T(8,128)(2,1)}, u32[]{:S(2)}) copy-start(bf16[2,512,512]{2,1,0:T(8,128)(2,1)} %object_ref.1) | copy-start | bytes 3145732
  2.5 11.8 %copy-start.1 = (f32[2,2,256,256]{3,2,1,0:T(8,128)S(1)}, f32[2,2,256,256]{3,2,1,0:T(8,128)}, u32[]{:S(2)}) copy-start(f32[2,2,256,256]{3,2,1,0:T(8,128)} %probe_ref.1) | copy-start | bytes 3145732
  2.5 11.8 %copy-start.2 = (bf16[1,1,8,256,256]{4,3,2,1,0:T(8,128)(2,1)S(1)}, bf16[1,1,8,256,256]{4,3,2,1,0:T(8,128)(2,1)}, u32[]{:S(2)}) copy-start(bf16[1,1,8,256,256]{4,3,2,1,0:T(8,128)(2,1)} %param.9) | copy-start | bytes 3145732
  2.5 11.8 %copy-start.3 = (bf16[256,256]{1,0:T(8,128)(2,1)S(1)}, bf16[256,256]{1,0:T(8,128)(2,1)}, u32[]{:S(2)}) copy-start(bf16[256,256]{1,0:T(8,128)(2,1)} %constant.10.ti_ref) | copy-start | bytes 393220
  2.5 11.8 %copy-start.4 = (bf16[256,256]{1,0:T(8,128)(2,1)S(1)}, bf16[256,256]{1,0:T(8,128)(2,1)}, u32[]{:S(2)}) copy-start(bf16[256,256]{1,0:T(8,128)(2,1)} %constant.9.tr_ref) | copy-start | bytes 393220

commit v4 on v3

--- a/solution.py
+++ b/solution.py
@@ -96,17 +96,21 @@
     for t in range(side_cols // LANES):
         ext_ref[:, HALO // LANES + t, HALO : HALO + side_rows, :] = object_ref[
             :, :, t * LANES : (t + 1) * LANES
-        ]
+        ].astype(jnp.float32)
+    spare = ext_ref.shape[1] - 1
+    ext_ref[:, spare] = jnp.zeros((2, ext_ref.shape[2], LANES), jnp.float32)
     for index, side in enumerate(SIDES):
         dr, dc = opposite(side)
         rows = part(dr, HALO, side_rows)
-        tiles = range(ext_ref.shape[1])[part(dc, HALO // LANES, side_cols // LANES)]
+        tiles = range(spare)[part(dc, HALO // LANES, side_cols // LANES)]
 
         @pl.when(exists((dr, dc)))
         def _(index=index, rows=rows, tiles=tiles):
             copy(index).wait_recv()
             for k, t in enumerate(tiles):
-                ext_ref[:, t, rows, :] = landings[index][:, :, k * LANES : (k + 1) * LANES]
+                ext_ref[:, t, rows, :] = landings[index][
+                    :, :, k * LANES : (k + 1) * LANES
+                ].astype(jnp.float32)
 
         @pl.when(jnp.logical_not(exists((dr, dc))))
         def _(rows=rows, tiles=tiles, index=index):
@@ -134,13 +138,13 @@
     return pl.pallas_call(
         halo_kernel,
         out_shape=jax.ShapeDtypeStruct(
-            (2, (side_cols + 2 * HALO) // LANES, side_rows + 2 * HALO, LANES), object_field.dtype
+            (2, (side_cols + 2 * HALO) // LANES + 1, side_rows + 2 * HALO, LANES), jnp.float32
         ),
         in_specs=[vmem],
         out_specs=vmem,
         scratch_shapes=landings + [sems, sems],
         compiler_params=pltpu.CompilerParams(
-            collective_id=0, has_side_effects=True, vmem_limit_bytes=10 * 1024 * 1024
+            collective_id=0, has_side_effects=True, vmem_limit_bytes=14 * 1024 * 1024
         ),
         name="halo",
     )(object_field)
@@ -372,18 +376,18 @@
 
 def frames_kernel(
     count_ref, at_ref, ext_ref, probe_ref, amp_ref, tr_ref, ti_ref, acc_ref, pacc_ref,
-    extf, fwd, inv, stage, half, wide, patch,
+    fwd, inv, *buffers,
 ):
     fs = probe_ref.shape[-1]
     modes = probe_ref.shape[1]
-    tiles = ext_ref.shape[1]
     lane_tiles = fs // LANES
-    for plane in range(2):
-        for t in range(tiles):
-            extf[plane, t] = ext_ref[plane, t].astype(jnp.float32)
-        extf[plane, tiles] = jnp.zeros(extf.shape[2:], jnp.float32)
+    last_slot = amp_ref.shape[0] - 1
+    live = count_ref[0]
+    even, odd = buffers[:4], buffers[4:]
     acc_ref[...] = jnp.zeros(acc_ref.shape, jnp.float32)
     pacc_ref[...] = jnp.zeros(pacc_ref.shape, jnp.float32)
+    odd[2][...] = jnp.zeros(odd[2].shape, jnp.float32)
+    odd[3][...] = jnp.zeros(odd[3].shape, jnp.float32)
     table_real, table_imag = tr_ref[...], ti_ref[...]
     minus = -table_imag
     fwd[:fs, :fs] = table_real
@@ -395,14 +399,16 @@
     inv[fs:, :fs] = minus
     inv[fs:, fs:] = table_real
 
-    def two_sided(left_table, right_table):
+    def two_sided(buffer, left_table, right_table):
+        stage, half, wide, _ = buffer
         for m in range(modes):
             both = dot32(left_table[...], stage[:, m * fs : (m + 1) * fs])
             half[m * fs : (m + 1) * fs, :fs] = both[:fs].astype(jnp.bfloat16)
             half[m * fs : (m + 1) * fs, fs:] = both[fs:].astype(jnp.bfloat16)
         wide[...] = dot32(half[...], right_table[...])
 
-    def advance(slot, carry):
+    def make_exit(buffer, slot):
+        stage, _, _, patch = buffer
         row_at = at_ref[0, slot]
         col_at = at_ref[1, slot]
         tile_at = col_at // LANES
@@ -410,14 +416,13 @@
         back_shift = (LANES - shift) % LANES
         lane = lax.broadcasted_iota(jnp.int32, (CHUNK, LANES), 1)
         keep_low = lane < LANES - shift
-        from_same = lane >= shift
         for r in range(0, fs, CHUNK):
             rows = slice(r, r + CHUNK)
             values = []
             for plane in range(2):
                 rolled = [
                     pltpu.roll(
-                        extf[plane, tile_at + t, pl.ds(row_at + r, CHUNK), :], back_shift, 1
+                        ext_ref[plane, tile_at + t, pl.ds(row_at + r, CHUNK), :], back_shift, 1
                     )
                     for t in range(lane_tiles + 1)
                 ]
@@ -439,25 +444,38 @@
                     stage[fs + r : fs + r + CHUNK, out] = (
                         probe_real * patch_imag + probe_imag * patch_real
                     ).astype(jnp.bfloat16)
-        two_sided(fwd, inv)
+
+    def make_chi(buffer, slot, valid):
+        stage, _, wide, _ = buffer
         for r in range(0, fs, CHUNK):
             for t in range(lane_tiles):
                 cols = slice(t * LANES, (t + 1) * LANES)
                 imag_cols = slice(fs + t * LANES, fs + (t + 1) * LANES)
                 psi = []
-                power = jnp.zeros((CHUNK, LANES), jnp.float32)
+                power = None
                 for m in range(modes):
                     rows = slice(m * fs + r, m * fs + r + CHUNK)
                     real, imag = wide[rows, cols], wide[rows, imag_cols]
                     psi.append((real, imag))
-                    power = power + (real * real + imag * imag)
+                    own = real * real + imag * imag
+                    power = own if power is None else power + own
                 amp = amp_ref[slot, r : r + CHUNK, cols].astype(jnp.float32)
                 factor = 1.0 - amp * lax.rsqrt(jnp.maximum(power, 0.25))
+                if valid is not None:
+                    factor = jnp.where(valid, factor, 0.0)
                 for m in range(modes):
                     out = slice(m * fs + t * LANES, m * fs + (t + 1) * LANES)
                     stage[r : r + CHUNK, out] = (psi[m][0] * factor).astype(jnp.bfloat16)
                     stage[fs + r : fs + r + CHUNK, out] = (psi[m][1] * factor).astype(jnp.bfloat16)
-        two_sided(inv, fwd)
+
+    def add_grads(buffer, slot):
+        _, _, wide, patch = buffer
+        row_at = at_ref[0, slot]
+        col_at = at_ref[1, slot]
+        tile_at = col_at // LANES
+        shift = col_at % LANES
+        lane = lax.broadcasted_iota(jnp.int32, (CHUNK, LANES), 1)
+        from_same = lane >= shift
         for r in range(0, fs, CHUNK):
             grads = [[], []]
             for t in range(lane_tiles):
@@ -465,14 +483,16 @@
                 imag_cols = slice(fs + t * LANES, fs + (t + 1) * LANES)
                 patch_real = patch[0, r : r + CHUNK, cols]
                 patch_imag = patch[1, r : r + CHUNK, cols]
-                total_real = total_imag = 0.0
+                total_real = total_imag = None
                 for m in range(modes):
                     rows = slice(m * fs + r, m * fs + r + CHUNK)
                     real, imag = wide[rows, cols], wide[rows, imag_cols]
                     probe_real = probe_ref[0, m, r : r + CHUNK, cols]
                     probe_imag = probe_ref[1, m, r : r + CHUNK, cols]
-                    total_real = total_real + (probe_real * real + probe_imag * imag)
-                    total_imag = total_imag + (probe_real * imag - probe_imag * real)
+                    own_real = probe_real * real + probe_imag * imag
+                    own_imag = probe_real * imag - probe_imag * real
+                    total_real = own_real if m == 0 else total_real + own_real
+                    total_imag = own_imag if m == 0 else total_imag + own_imag
                     at = (m * lane_tiles + t) * fs + r
                     pacc_ref[at : at + CHUNK, :] += patch_real * real + patch_imag * imag
                     at += modes * lane_tiles * fs
@@ -486,15 +506,31 @@
                     before = rolled[t - 1] if t > 0 else 0.0
                     where = (plane, tile_at + t, pl.ds(row_at + r, CHUNK), slice(None))
                     acc_ref[where] += jnp.where(from_same, same, before)
+
+    def advance(pair, carry):
+        first = 2 * pair
+        second = jnp.minimum(first + 1, last_slot)
+        make_exit(even, first)
+        two_sided(even, fwd, inv)
+        add_grads(odd, jnp.maximum(first - 1, 0))
+        make_exit(odd, second)
+        two_sided(odd, fwd, inv)
+        make_chi(even, first, None)
+        two_sided(even, inv, fwd)
+        make_chi(odd, second, first + 1 < live)
+        two_sided(odd, inv, fwd)
+        add_grads(even, first)
         return carry
 
-    lax.fori_loop(0, count_ref[0], advance, 0)
+    pairs = (live + 1) // 2
+    lax.fori_loop(0, pairs, advance, 0)
+    add_grads(odd, jnp.minimum(2 * pairs - 1, last_slot))
 
 
 def frames_call(extended, probe_modes, amplitudes, positions, live_count, tables):
     fs = probe_modes.shape[-1]
     modes = probe_modes.shape[1]
-    tiled = (2, extended.shape[1] + 1, extended.shape[2], LANES)
+    tiled = extended.shape
     vmem = pl.BlockSpec(memory_space=pltpu.VMEM)
     smem = pl.BlockSpec(memory_space=pltpu.SMEM)
     return pl.pallas_call(
@@ -506,9 +542,11 @@
         in_specs=[smem, smem, vmem, vmem, vmem, vmem, vmem],
         out_specs=(vmem, vmem),
         scratch_shapes=[
-            pltpu.VMEM(tiled, jnp.float32),
             pltpu.VMEM((2 * fs, 2 * fs), jnp.bfloat16),
             pltpu.VMEM((2 * fs, 2 * fs), jnp.bfloat16),
+        ]
+        + 2
+        * [
             pltpu.VMEM((2 * fs, modes * fs), jnp.bfloat16),
             pltpu.VMEM((modes * fs, 2 * fs), jnp.bfloat16),
             pltpu.VMEM((modes * fs, 2 * fs), jnp.float32),

time: 66.3 us -> 61 us (0.920)
  Pallas kernels: 61 us -> 56.2 us
    pallas_call x1, Pallas kernels: 36.9 us -> 33.2 us  [reduce_call(): pl.pallas_call(functools.partial(reduce_kernel, scale), out_shape=(jax.Sh...]
    pallas_call x1, Pallas kernels: 12.4 us -> 11.2 us  [frames_call(): pl.pallas_call(frames_kernel, out_shape=(jax.ShapeDtypeStruct(tiled, jnp....]
where the time goes in v4:
time: 61 us; the launch traced here: 61.1 us
  Pallas kernels  56.2 us (92%)
  local copies, waits for them, and re-layouts  3.53 us (6%)
  between operations  1.37 us (2%)
    pallas_call x1, Pallas kernels, reduce_call(): pl.pallas_call(functools.partial(reduce_kernel, scale), out_shape=(jax.Sh...  33.2 us
    pallas_call x1, Pallas kernels, halo_call(): pl.pallas_call(halo_kernel, out_shape=jax.ShapeDtypeStruct((2, (side_cols...  11.8 us
    pallas_call x1, Pallas kernels, frames_call(): pl.pallas_call(frames_kernel, out_shape=(jax.ShapeDtypeStruct(tiled, jnp....  11.2 us
    unnamed x14, local copies, waits for them, and re-layouts  3.53 us

profile of v4, /device:TPU:0, one launch (start us, length us, event | category | flops | bytes accessed | tf_op | source)
XLA Modules:
  0.0 61.1 jit_solution(17557985098751563139)
XLA Ops:
  0.6 0.0 copy-start.5
  1.3 0.0 copy-start
  1.3 1.2 %copy-done = bf16[2,512,512]{2,1,0:T(8,128)(2,1)S(1)} copy-done((bf16[2,512,512]{2,1,0:T(8,128)(2,1)S(1)}, bf16[2,512,512]{2,1,0:T(8,128)(2,1)}, u32[]{:S(2)}) %copy-start) | copy-done | bytes 1048600
  2.5 0.0 copy-start.1
  2.5 0.0 copy-start.2
  2.5 0.0 copy-start.3
  2.5 0.0 copy-start.4
  2.5 11.8 %halo.1.ext_ref = f32[2,7,768,128]{3,2,1,0:T(8,128)S(1)} custom-call(bf16[2,512,512]{2,1,0:T(8,128)(2,1)S(1)} %copy-done), custom_call_target="tpu_custom_call" | custom-call | tf_op jit(solution)/shard_map/halo/pallas_call | solution.py:138
  14.3 0.0 copy-done.5
  14.3 0.0 copy-done.1
  14.4 0.0 copy-done.2
  14.4 0.0 copy-done.3
  14.4 0.0 copy-done.4
  14.4 11.2 %frames.1 = (f32[2,7,768,128]{3,2,1,0:T(8,128)S(1)}, f32[2048,128]{1,0:T(8,128)S(1)}) custom-call(s32[1]{0:T(128)} %bitcast.3.count_ref, s32[2,8]{1,0:T(2,128)S(1)} %bitcast.5, f32[2,7,768,128]{3,2,1,0:T(8,128)S(1)} %halo.1.ext_ref, f32[2,2,256,256]{3,2,1,0:T(8,128)S(1)} %copy-done.1, bf16[8,256,256]{2,1,0:T(8,128)(2,1)S(1)} %bitcast.4, ...), custom_call_target="tpu_custom_call" | custom-call | tf_op jit(solution)/shard_map/frames/pallas_call | solution.py:536
  25.6 33.2 %reduce.1 = (f32[2,512,512]{2,1,0:T(8,128)S(1)}, f32[2,2,256,256]{3,2,1,0:T(8,128)S(1)}) custom-call(f32[2,7,768,128]{3,2,1,0:T(8,128)S(1)} %get-tuple-element.4.acc_ref, f32[2048,128]{1,0:T(8,128)S(1)} %get-tuple-element.5.pacc_ref), custom_call_target="tpu_custom_call" | custom-call | tf_op jit(solution)/shard_map/reduce/pallas_call | solution.py:332
  58.8 1.3 %copy.12 = f32[2,512,512]{2,1,0:T(8,128)} copy(f32[2,512,512]{2,1,0:T(8,128)S(1)} %get-tuple-element.8) | data formatting | bytes 4194304
  60.1 1.0 %copy.13 = f32[2,2,256,256]{3,2,1,0:T(8,128)} copy(f32[2,2,256,256]{3,2,1,0:T(8,128)S(1)} %get-tuple-element.9) | data formatting | bytes 2097152
Async XLA Ops:
  0.6 13.7 %copy-start.5 = (s32[1,1,2,8]{3,2,1,0:T(2,128)S(1)}, s32[1,1,2,8]{3,2,1,0:T(2,128)}, u32[]{:S(2)}) copy-start(s32[1,1,2,8]{3,2,1,0:T(2,128)} %param.10) | copy-start | bytes 196
  1.3 1.2 %copy-start = (bf16[2,512,512]{2,1,0:T(8,128)(2,1)S(1)}, bf16[2,512,512]{2,1,0:T(8,128)(2,1)}, u32[]{:S(2)}) copy-start(bf16[2,512,512]{2,1,0:T(8,128)(2,1)} %object_ref.1) | copy-start | bytes 3145732
  2.5 11.8 %copy-start.1 = (f32[2,2,256,256]{3,2,1,0:T(8,128)S(1)}, f32[2,2,256,256]{3,2,1,0:T(8,128)}, u32[]{:S(2)}) copy-start(f32[2,2,256,256]{3,2,1,0:T(8,128)} %probe_ref.1) | copy-start | bytes 3145732
  2.5 11.8 %copy-start.2 = (bf16[1,1,8,256,256]{4,3,2,1,0:T(8,128)(2,1)S(1)}, bf16[1,1,8,256,256]{4,3,2,1,0:T(8,128)(2,1)}, u32[]{:S(2)}) copy-start(bf16[1,1,8,256,256]{4,3,2,1,0:T(8,128)(2,1)} %param.9) | copy-start | bytes 3145732
  2.5 11.8 %copy-start.3 = (bf16[256,256]{1,0:T(8,128)(2,1)S(1)}, bf16[256,256]{1,0:T(8,128)(2,1)}, u32[]{:S(2)}) copy-start(bf16[256,256]{1,0:T(8,128)(2,1)} %constant.10.ti_ref) | copy-start | bytes 393220
  2.5 11.8 %copy-start.4 = (bf16[256,256]{1,0:T(8,128)(2,1)S(1)}, bf16[256,256]{1,0:T(8,128)(2,1)}, u32[]{:S(2)}) copy-start(bf16[256,256]{1,0:T(8,128)(2,1)} %constant.9.tr_ref) | copy-start | bytes 393220

commit v5 on v4

--- a/solution.py
+++ b/solution.py
@@ -153,7 +153,8 @@
 def reduce_kernel(scale, acc_ref, pacc_ref, grad_ref, probe_ref, *scratch):
     count = len(SIDES)
     sends, landings, rest = scratch[:count], scratch[count : 2 * count], scratch[2 * count :]
-    psend, precv, zsend, zrecv, full, side_sems, col_sems, row_sems = rest
+    psend, pair_recv, merged, precv, zsend, zrecv, full = rest[:7]
+    side_sems, pair_sems, col_sems, row_sems = rest[7:]
     row, col, n_row, n_col = position()
     side_rows, side_cols = grad_ref.shape[1:]
     margin = HALO // LANES
@@ -187,6 +188,9 @@
 
     share = psend.shape[0] // n_col
     piece = share // n_row
+    chip, core = col // 2, lax.rem(col, 2)
+    n_chip = n_col // 2
+    sibling = (row, 2 * chip + 1 - core)
 
     def to_peer(source, landing, sems, which, k, device):
         return pltpu.make_async_remote_copy(
@@ -198,8 +202,14 @@
             device_id_type=MESH,
         )
 
-    def col_peer(k):
-        return (row, lax.rem(col + k, n_col))
+    def chip_at(k):
+        return lax.rem(chip + k, n_chip)
+
+    def chip_from(k):
+        return lax.rem(chip + n_chip - k, n_chip)
+
+    def chip_peer(k):
+        return (row, 2 * chip_at(k) + core)
 
     def row_peer(k):
         return (lax.rem(row + k, n_row), col)
@@ -207,10 +217,12 @@
     def share_of(ref, index):
         return ref.at[pl.ds(pl.multiple_of(index * share, share), share)]
 
+    def pair_copy(k):
+        source = share_of(psend, 2 * chip_at(k) + 1 - core)
+        return to_peer(source, pair_recv.at[k], pair_sems, 0, k + 1, sibling)
+
     def scatter_copy(k):
-        return to_peer(
-            share_of(psend, lax.rem(col + k, n_col)), precv.at[k - 1], col_sems, 0, k, col_peer(k)
-        )
+        return to_peer(merged.at[k - 1], precv.at[k - 1], col_sems, 0, k, chip_peer(k))
 
     def row_scatter_copy(k):
         target = lax.rem(row + k, n_row)
@@ -231,15 +243,21 @@
         return to_peer(piece_of(row), piece_of(owner), row_sems, 2, k, row_peer(k))
 
     def gather_copy(k, owner):
-        return to_peer(share_of(full, col), share_of(full, owner), col_sems, 2, k, col_peer(k))
+        return to_peer(share_of(full, col), share_of(full, owner), col_sems, 2, k, chip_peer(k))
+
+    def forward_copy(k, side):
+        source = share_of(full, 2 * chip_from(k) + core)
+        landing = share_of(full, 2 * chip_from(k) + side)
+        return to_peer(source, landing, pair_sems, 2, k + 1, sibling)
 
     def side_copy(index):
         return to_side(
             SIDES[index], index, sends[index], landings[index], side_sems.at[0], side_sems.at[1]
         )
 
-    for k in range(1, n_col):
-        scatter_copy(k).start()
+    order = list(range(1, n_chip)) + [0]
+    for k in order:
+        pair_copy(k).start()
 
     def start_sides(chosen):
         for index, side in enumerate(SIDES):
@@ -250,12 +268,21 @@
                     side_copy(index).start()
 
     start_sides(lambda side: side[1] == 0)
+    def merge(k):
+        pair_copy(k).wait_recv()
+        index = 2 * chip_at(k) + core
+        own = pacc_ref[pl.ds(pl.multiple_of(index * share, share), share), :]
+        return own + pair_recv[k].astype(jnp.float32)
+
+    for k in range(1, n_chip):
+        merged[k - 1] = merge(k).astype(jnp.bfloat16)
+        scatter_copy(k).start()
+    total = merge(0)
     for t in range(inner):
         grad_ref[:, :, t * LANES : (t + 1) * LANES] = acc_ref[
             :, margin + t, HALO : HALO + side_rows, :
         ]
-    total = pacc_ref[pl.ds(pl.multiple_of(col * share, share), share), :]
-    for k in range(1, n_col):
+    for k in range(1, n_chip):
         scatter_copy(k).wait_recv()
         total = total + precv[k - 1].astype(jnp.float32)
     zsend[...] = total
@@ -273,8 +300,12 @@
         row_gather_copy(k, row).start()
     for k in range(1, n_row):
         row_gather_copy(k, lax.rem(row + n_row - k, n_row)).wait_recv()
-    for k in range(1, n_col):
+    for k in range(1, n_chip):
         gather_copy(k, col).start()
+    forward_copy(0, core).start()
+    for k in range(1, n_chip):
+        gather_copy(k, 2 * chip_from(k) + core).wait_recv()
+        forward_copy(k, core).start()
 
     for index, side in enumerate(SIDES):
         dr, dc = opposite(side)
@@ -289,8 +320,8 @@
                     jnp.float32
                 )
 
-    for k in range(1, n_col):
-        gather_copy(k, lax.rem(col + n_col - k, n_col)).wait_recv()
+    for k in range(n_chip):
+        forward_copy(k, 1 - core).wait_recv()
     parts, modes, fs, width = probe_ref.shape
     at = 0
     for p in range(parts):
@@ -300,9 +331,12 @@
                     jnp.float32
                 )
                 at += fs
-    for k in range(1, n_col):
+    for k in range(1, n_chip):
         scatter_copy(k).wait_send()
         gather_copy(k, col).wait_send()
+    for k in range(n_chip):
+        pair_copy(k).wait_send()
+        forward_copy(k, core).wait_send()
     for k in range(1, n_row):
         row_scatter_copy(k).wait_send()
         row_gather_copy(k, row).wait_send()
@@ -329,6 +363,7 @@
     total_rows = probe_flat.shape[0]
     share = total_rows // n_col
     piece = share // n_row
+    n_chip = n_col // 2
     return pl.pallas_call(
         functools.partial(reduce_kernel, scale),
         out_shape=(
@@ -341,12 +376,15 @@
         + buffers
         + [
             pltpu.VMEM((total_rows, LANES), jnp.bfloat16),
-            pltpu.VMEM((n_col - 1, share, LANES), jnp.bfloat16),
+            pltpu.VMEM((n_chip, share, LANES), jnp.bfloat16),
+            pltpu.VMEM((n_chip - 1, share, LANES), jnp.bfloat16),
+            pltpu.VMEM((n_chip - 1, share, LANES), jnp.bfloat16),
             pltpu.VMEM((share, LANES), jnp.float32),
             pltpu.VMEM((n_row - 1, piece, LANES), jnp.float32),
             pltpu.VMEM((total_rows, LANES), jnp.bfloat16),
             pltpu.SemaphoreType.DMA((2, len(SIDES))),
-            pltpu.SemaphoreType.DMA((4, n_col - 1)),
+            pltpu.SemaphoreType.DMA((4, n_chip)),
+            pltpu.SemaphoreType.DMA((4, n_chip - 1)),
             pltpu.SemaphoreType.DMA((4, n_row - 1)),
         ],
         compiler_params=pltpu.CompilerParams(

time: 61 us -> 58.6 us (0.961)
  Pallas kernels: 56.2 us -> 53.7 us
    pallas_call x1, Pallas kernels: 11.2 us -> 8.03 us  [frames_call(): pl.pallas_call(frames_kernel, out_shape=(jax.ShapeDtypeStruct(tiled, jnp....]
    pallas_call x1, Pallas kernels: 33.2 us -> 33.9 us  [reduce_call(): pl.pallas_call(functools.partial(reduce_kernel, scale), out_shape=(jax.Sh...]
where the time goes in v5:
time: 58.6 us
  Pallas kernels  53.7 us (92%)
  local copies, waits for them, and re-layouts  3.53 us (6%)
  between operations  1.37 us (2%)
    pallas_call x1, Pallas kernels, reduce_call(): pl.pallas_call(functools.partial(reduce_kernel, scale), out_shape=(jax.Sh...  33.9 us
    pallas_call x1, Pallas kernels, halo_call(): pl.pallas_call(halo_kernel, out_shape=jax.ShapeDtypeStruct((2, (side_cols...  11.8 us
    pallas_call x1, Pallas kernels, frames_call(): pl.pallas_call(frames_kernel, out_shape=(jax.ShapeDtypeStruct(tiled, jnp....  8.03 us
    unnamed x14, local copies, waits for them, and re-layouts  3.53 us

profile of v5, /device:TPU:0, one launch (start us, length us, event | category | flops | bytes accessed | tf_op | source)
XLA Modules:
  0.0 58.6 jit_solution(9202111417043546314)
XLA Ops:
  0.6 0.0 copy-start.5
  1.3 0.0 copy-start
  1.3 1.2 %copy-done = bf16[2,512,512]{2,1,0:T(8,128)(2,1)S(1)} copy-done((bf16[2,512,512]{2,1,0:T(8,128)(2,1)S(1)}, bf16[2,512,512]{2,1,0:T(8,128)(2,1)}, u32[]{:S(2)}) %copy-start) | copy-done | bytes 1048600
  2.5 0.0 copy-start.1
  2.5 0.0 copy-start.2
  2.5 0.0 copy-start.3
  2.5 0.0 copy-start.4
  2.5 11.8 %halo.1.ext_ref = f32[2,7,768,128]{3,2,1,0:T(8,128)S(1)} custom-call(bf16[2,512,512]{2,1,0:T(8,128)(2,1)S(1)} %copy-done), custom_call_target="tpu_custom_call" | custom-call | tf_op jit(solution)/shard_map/halo/pallas_call | solution.py:138
  14.3 0.0 copy-done.5
  14.3 0.0 copy-done.1
  14.4 0.0 copy-done.2
  14.4 0.0 copy-done.3
  14.4 0.0 copy-done.4
  14.4 8.0 %frames.1 = (f32[2,7,768,128]{3,2,1,0:T(8,128)S(1)}, f32[2048,128]{1,0:T(8,128)S(1)}) custom-call(s32[1]{0:T(128)} %bitcast.3.count_ref, s32[2,8]{1,0:T(2,128)S(1)} %bitcast.5, f32[2,7,768,128]{3,2,1,0:T(8,128)S(1)} %halo.1.ext_ref, f32[2,2,256,256]{3,2,1,0:T(8,128)S(1)} %copy-done.1, bf16[8,256,256]{2,1,0:T(8,128)(2,1)S(1)} %bitcast.4, ...), custom_call_target="tpu_custom_call" | custom-call | tf_op jit(solution)/shard_map/frames/pallas_call | solution.py:574
  22.4 33.9 %reduce.1 = (f32[2,512,512]{2,1,0:T(8,128)S(1)}, f32[2,2,256,256]{3,2,1,0:T(8,128)S(1)}) custom-call(f32[2,7,768,128]{3,2,1,0:T(8,128)S(1)} %get-tuple-element.4.acc_ref, f32[2048,128]{1,0:T(8,128)S(1)} %get-tuple-element.5.pacc_ref), custom_call_target="tpu_custom_call" | custom-call | tf_op jit(solution)/shard_map/reduce/pallas_call | solution.py:367
  56.3 1.3 %copy.12 = f32[2,512,512]{2,1,0:T(8,128)} copy(f32[2,512,512]{2,1,0:T(8,128)S(1)} %get-tuple-element.8) | data formatting | bytes 4194304
  57.6 1.0 %copy.13 = f32[2,2,256,256]{3,2,1,0:T(8,128)} copy(f32[2,2,256,256]{3,2,1,0:T(8,128)S(1)} %get-tuple-element.9) | data formatting | bytes 2097152
Async XLA Ops:
  0.6 13.7 %copy-start.5 = (s32[1,1,2,8]{3,2,1,0:T(2,128)S(1)}, s32[1,1,2,8]{3,2,1,0:T(2,128)}, u32[]{:S(2)}) copy-start(s32[1,1,2,8]{3,2,1,0:T(2,128)} %param.10) | copy-start | bytes 196
  1.3 1.2 %copy-start = (bf16[2,512,512]{2,1,0:T(8,128)(2,1)S(1)}, bf16[2,512,512]{2,1,0:T(8,128)(2,1)}, u32[]{:S(2)}) copy-start(bf16[2,512,512]{2,1,0:T(8,128)(2,1)} %object_ref.1) | copy-start | bytes 3145732
  2.5 11.8 %copy-start.1 = (f32[2,2,256,256]{3,2,1,0:T(8,128)S(1)}, f32[2,2,256,256]{3,2,1,0:T(8,128)}, u32[]{:S(2)}) copy-start(f32[2,2,256,256]{3,2,1,0:T(8,128)} %probe_ref.1) | copy-start | bytes 3145732
  2.5 11.8 %copy-start.2 = (bf16[1,1,8,256,256]{4,3,2,1,0:T(8,128)(2,1)S(1)}, bf16[1,1,8,256,256]{4,3,2,1,0:T(8,128)(2,1)}, u32[]{:S(2)}) copy-start(bf16[1,1,8,256,256]{4,3,2,1,0:T(8,128)(2,1)} %param.9) | copy-start | bytes 3145732
  2.5 11.8 %copy-start.3 = (bf16[256,256]{1,0:T(8,128)(2,1)S(1)}, bf16[256,256]{1,0:T(8,128)(2,1)}, u32[]{:S(2)}) copy-start(bf16[256,256]{1,0:T(8,128)(2,1)} %constant.10.ti_ref) | copy-start | bytes 393220
  2.5 11.8 %copy-start.4 = (bf16[256,256]{1,0:T(8,128)(2,1)S(1)}, bf16[256,256]{1,0:T(8,128)(2,1)}, u32[]{:S(2)}) copy-start(bf16[256,256]{1,0:T(8,128)(2,1)} %constant.9.tr_ref) | copy-start | bytes 393220

commit v6 on v5

--- a/solution.py
+++ b/solution.py
@@ -68,8 +68,11 @@
     )
 
 
-def halo_kernel(object_ref, ext_ref, *scratch):
-    landings, (send_sems, recv_sems) = scratch[: len(SIDES)], scratch[len(SIDES) :]
+def halo_kernel(whole_ref, ext_ref, *scratch):
+    landings, (send_sems, recv_sems) = scratch[: len(SIDES)], scratch[len(SIDES) : -2]
+    object_ref, load_sem = scratch[-2:]
+    load = pltpu.make_async_copy(whole_ref, object_ref, load_sem)
+    load.start()
     side_rows, side_cols = object_ref.shape[1:]
     barrier = pltpu.get_barrier_semaphore()
     count = jnp.int32(0)
@@ -81,6 +84,7 @@
 
         count = count + exists(side).astype(jnp.int32)
     pl.semaphore_wait(barrier, count)
+    load.wait()
 
     def copy(index):
         dr, dc = SIDES[index]
@@ -140,9 +144,10 @@
         out_shape=jax.ShapeDtypeStruct(
             (2, (side_cols + 2 * HALO) // LANES + 1, side_rows + 2 * HALO, LANES), jnp.float32
         ),
-        in_specs=[vmem],
+        in_specs=[pl.BlockSpec(memory_space=pltpu.HBM)],
         out_specs=vmem,
-        scratch_shapes=landings + [sems, sems],
+        scratch_shapes=landings
+        + [sems, sems, pltpu.VMEM(object_field.shape, object_field.dtype), pltpu.SemaphoreType.DMA],
         compiler_params=pltpu.CompilerParams(
             collective_id=0, has_side_effects=True, vmem_limit_bytes=14 * 1024 * 1024
         ),

time: 58.6 us -> 58.5 us (level)
    pallas_call x1, Pallas kernels: 33.9 us -> 27 us  [reduce_call(): pl.pallas_call(functools.partial(reduce_kernel, scale), out_shape=(jax.Sh...]
    pallas_call x1, Pallas kernels: 8.03 us -> 14.4 us  [frames_call(): pl.pallas_call(frames_kernel, out_shape=(jax.ShapeDtypeStruct(tiled, jnp....]
where the time goes in v6:
time: 58.5 us; the launch traced here: 58.2 us
  Pallas kernels  53.3 us (91%)
  local copies, waits for them, and re-layouts  3.53 us (6%)
  between operations  1.37 us (2%)
    pallas_call x1, Pallas kernels, reduce_call(): pl.pallas_call(functools.partial(reduce_kernel, scale), out_shape=(jax.Sh...  27 us
    pallas_call x1, Pallas kernels, frames_call(): pl.pallas_call(frames_kernel, out_shape=(jax.ShapeDtypeStruct(tiled, jnp....  14.4 us
    pallas_call x1, Pallas kernels, halo_call(): pl.pallas_call(halo_kernel, out_shape=jax.ShapeDtypeStruct((2, (side_cols...  11.9 us
    unnamed x14, local copies, waits for them, and re-layouts  3.53 us

profile of v6, /device:TPU:0, one launch (start us, length us, event | category | flops | bytes accessed | tf_op | source)
XLA Modules:
  0.0 58.2 jit_solution(12796271408077137177)
XLA Ops:
  0.6 0.0 copy-start.5
  1.3 0.0 copy-start
  1.3 1.2 %copy-done = bf16[2,512,512]{2,1,0:T(8,128)(2,1)S(1)} copy-done((bf16[2,512,512]{2,1,0:T(8,128)(2,1)S(1)}, bf16[2,512,512]{2,1,0:T(8,128)(2,1)}, u32[]{:S(2)}) %copy-start) | copy-done | bytes 1048600
  2.5 0.0 copy-start.1
  2.5 0.0 copy-start.2
  2.5 0.0 copy-start.3
  2.5 0.0 copy-start.4
  2.5 11.9 %halo.1.ext_ref = f32[2,7,768,128]{3,2,1,0:T(8,128)S(1)} custom-call(bf16[2,512,512]{2,1,0:T(8,128)(2,1)S(1)} %copy-done), custom_call_target="tpu_custom_call" | custom-call | tf_op jit(solution)/shard_map/halo/pallas_call | solution.py:142
  14.4 0.0 copy-done.5
  14.4 0.0 copy-done.1
  14.4 0.0 copy-done.2
  14.4 0.0 copy-done.3
  14.5 0.0 copy-done.4
  14.5 14.4 %frames.1 = (f32[2,7,768,128]{3,2,1,0:T(8,128)S(1)}, f32[2048,128]{1,0:T(8,128)S(1)}) custom-call(s32[1]{0:T(128)} %bitcast.3.count_ref, s32[2,8]{1,0:T(2,128)S(1)} %bitcast.5, f32[2,7,768,128]{3,2,1,0:T(8,128)S(1)} %halo.1.ext_ref, f32[2,2,256,256]{3,2,1,0:T(8,128)S(1)} %copy-done.1, bf16[8,256,256]{2,1,0:T(8,128)(2,1)S(1)} %bitcast.4, ...), custom_call_target="tpu_custom_call" | custom-call | tf_op jit(solution)/shard_map/frames/pallas_call | solution.py:579
  28.9 27.0 %reduce.1 = (f32[2,512,512]{2,1,0:T(8,128)S(1)}, f32[2,2,256,256]{3,2,1,0:T(8,128)S(1)}) custom-call(f32[2,7,768,128]{3,2,1,0:T(8,128)S(1)} %get-tuple-element.4.acc_ref, f32[2048,128]{1,0:T(8,128)S(1)} %get-tuple-element.5.pacc_ref), custom_call_target="tpu_custom_call" | custom-call | tf_op jit(solution)/shard_map/reduce/pallas_call | solution.py:372
  55.9 1.3 %copy.12 = f32[2,512,512]{2,1,0:T(8,128)} copy(f32[2,512,512]{2,1,0:T(8,128)S(1)} %get-tuple-element.8) | data formatting | bytes 4194304
  57.2 1.0 %copy.13 = f32[2,2,256,256]{3,2,1,0:T(8,128)} copy(f32[2,2,256,256]{3,2,1,0:T(8,128)S(1)} %get-tuple-element.9) | data formatting | bytes 2097152
Async XLA Ops:
  0.6 13.8 %copy-start.5 = (s32[1,1,2,8]{3,2,1,0:T(2,128)S(1)}, s32[1,1,2,8]{3,2,1,0:T(2,128)}, u32[]{:S(2)}) copy-start(s32[1,1,2,8]{3,2,1,0:T(2,128)} %param.10) | copy-start | bytes 196
  1.3 1.2 %copy-start = (bf16[2,512,512]{2,1,0:T(8,128)(2,1)S(1)}, bf16[2,512,512]{2,1,0:T(8,128)(2,1)}, u32[]{:S(2)}) copy-start(bf16[2,512,512]{2,1,0:T(8,128)(2,1)} %whole_ref.1) | copy-start | bytes 3145732
  2.5 11.9 %copy-start.1 = (f32[2,2,256,256]{3,2,1,0:T(8,128)S(1)}, f32[2,2,256,256]{3,2,1,0:T(8,128)}, u32[]{:S(2)}) copy-start(f32[2,2,256,256]{3,2,1,0:T(8,128)} %probe_ref.1) | copy-start | bytes 3145732
  2.5 11.9 %copy-start.2 = (bf16[1,1,8,256,256]{4,3,2,1,0:T(8,128)(2,1)S(1)}, bf16[1,1,8,256,256]{4,3,2,1,0:T(8,128)(2,1)}, u32[]{:S(2)}) copy-start(bf16[1,1,8,256,256]{4,3,2,1,0:T(8,128)(2,1)} %param.9) | copy-start | bytes 3145732
  2.5 11.9 %copy-start.3 = (bf16[256,256]{1,0:T(8,128)(2,1)S(1)}, bf16[256,256]{1,0:T(8,128)(2,1)}, u32[]{:S(2)}) copy-start(bf16[256,256]{1,0:T(8,128)(2,1)} %constant.10.ti_ref) | copy-start | bytes 393220
  2.5 11.9 %copy-start.4 = (bf16[256,256]{1,0:T(8,128)(2,1)S(1)}, bf16[256,256]{1,0:T(8,128)(2,1)}, u32[]{:S(2)}) copy-start(bf16[256,256]{1,0:T(8,128)(2,1)} %constant.9.tr_ref) | copy-start | bytes 393220
